TPU v7x, 768 devices: a whole 4x8x12 slice. The times are simulated.
768 devices in a mesh: blocks: 64 (over y, x, core), group: 12 (over z).
Axes of the slice: x: 4, y: 8, z: 12, core: 2. Of those that a mesh axis runs over, the one named last changes fastest.
Arguments:
- ocean_state: float32 [36, 4, 512, 1536], P(None, None, 'blocks', 'group'), may hold values from -6 to 6
- surface_height: float32 [512, 1536], P('blocks', 'group'), may hold values from -6 to 6
- surface_damping: float32 [512, 1536], P('blocks', 'group'), may hold values from 0.05 to 1
- land_mask: int32 [512, 1536], P('blocks', 'group'), may hold values from 0 to 1, as said below
Outputs:
- new_state: float32 [36, 4, 512, 1536], P(None, None, 'blocks', 'group')
- surface: float32 [512, 1536], P('blocks', 'group')
Inputs may be any that keep to these rules, and one draw needn't show every extreme that they name: `land_mask`: 1 marks an ocean cell.
All inputs are finite; a program needn't handle non-finite values.
Results may differ from a plain program's by a relative error of at most 0.0003.
Values sent between devices are 32-bit elements; how exact they have to be, the bound alone decides.
A program may use at most 32 MiB of HBM per device.

v0:
```python
import jax
import jax.numpy as jnp
from jax import lax
from jax.sharding import PartitionSpec as P

ITERS = 3


time_step = 0.25
hyper_visc = 0.025
mixing = 0.2
gravity = 4.0
rotation = 0.2


def padded_2(shard, sides, width):
    for axis, dim in sides:
        count, length = (lax.axis_size(axis), shard.shape[dim])
        up = [(i, (i + 1) % count) for i in range(count - 1)]
        down = [(j, i) for i, j in up]
        last = lax.slice_in_dim(shard, length - width, length, axis=dim)
        initial = lax.slice_in_dim(shard, 0, width, axis=dim)
        before = lax.ppermute(last, axis, up)
        after = lax.ppermute(initial, axis, down)
        shard = jnp.concatenate([before, shard, after], axis=dim)
    return shard


def laplace(padded):
    return (
        padded[..., 2:, 1:-1]
        + padded[..., :-2, 1:-1]
        + padded[..., 1:-1, 2:]
        + padded[..., 1:-1, :-2]
        - 4.0 * padded[..., 1:-1, 1:-1]
    )


def on_device(ocean_state, surface_height, surface_damping, land_mask):
    sea_mask = land_mask.astype(jnp.float32)
    masked = ocean_state * sea_mask
    rows_dev, cols_dev = sea_mask.shape
    total_rows = rows_dev * lax.axis_size("blocks")
    total_cols = cols_dev * lax.axis_size("group")
    first_row = lax.axis_index("blocks") * rows_dev
    first_col = lax.axis_index("group") * cols_dev
    padded = padded_2(masked, (("blocks", 2), ("group", 3)), 2)
    lap_cycle = laplace(padded)
    row_pos = first_row - 1 + jnp.arange(rows_dev + 2, dtype=jnp.int32)
    col_pos = first_col - 1 + jnp.arange(cols_dev + 2, dtype=jnp.int32)
    inside = ((row_pos >= 0) & (row_pos < total_rows))[:, None] & (
        (col_pos >= 0) & (col_pos < total_cols)
    )[None, :]
    biharm = laplace(jnp.where(inside, lap_cycle, 0.0))
    near_cycle = padded[..., 1:-1, 1:-1]
    slope_east = 0.5 * (near_cycle[..., 2:, 1:-1] - near_cycle[..., :-2, 1:-1])
    slope_north = 0.5 * (near_cycle[..., 1:-1, 2:] - near_cycle[..., 1:-1, :-2])
    east_flow = masked[:, 2:3]
    north_flow = masked[:, 3:4]
    advect = east_flow * slope_east + north_flow * slope_north
    above_level = jnp.concatenate([masked[:1], masked[:-1]], axis=0)
    below_level = jnp.concatenate([masked[1:], masked[-1:]], axis=0)
    vertical = above_level + below_level - 2.0 * masked
    col_index = (first_col + jnp.arange(cols_dev, dtype=jnp.int32)).astype(jnp.float32)
    coriolis = rotation * (2.0 * (col_index + 0.5) / total_cols - 1.0)
    zeros_two = jnp.zeros_like(masked[:, 0:2])
    rotated = jnp.concatenate([zeros_two, coriolis * north_flow, -coriolis * east_flow], axis=1)
    updated = masked + time_step * (rotated - advect) - hyper_visc * biharm + mixing * vertical
    new_state = sea_mask * updated
    transport = jnp.sum(new_state[:, 2:4], axis=0) / new_state.shape[0]
    surface_pad = padded_2(transport, (("blocks", 1), ("group", 2)), 1)
    divergence = 0.5 * (
        surface_pad[0, 2:, 1:-1]
        - surface_pad[0, :-2, 1:-1]
        + surface_pad[1, 1:-1, 2:]
        - surface_pad[1, 1:-1, :-2]
    )
    right_side = sea_mask * (surface_damping * surface_height - gravity * divergence)
    solution = jnp.zeros_like(right_side)

    def global_total(value):
        part_sum = lax.psum(value, "blocks")
        return lax.psum(part_sum, "group")

    residual = right_side
    direction = right_side
    norm_now = global_total(jnp.sum(residual * residual))
    for iteration in range(ITERS):
        padded_field = padded_2(direction, (("blocks", 0), ("group", 1)), 1)
        beside = (
            padded_field[2:, 1:-1]
            + padded_field[:-2, 1:-1]
            + padded_field[1:-1, 2:]
            + padded_field[1:-1, :-2]
        )
        applied = sea_mask * ((4.0 + surface_damping) * direction - beside)
        step_size = norm_now / global_total(jnp.sum(direction * applied))
        solution = solution + step_size * direction
        if iteration + 1 < ITERS:
            residual = residual - step_size * applied
            norm_next = global_total(jnp.sum(residual * residual))
            direction = residual + norm_next / norm_now * direction
            norm_now = norm_next
    return (new_state, solution)


def solution(mesh):
    placed = (
        P(None, None, "blocks", "group"),
        P("blocks", "group"),
        P("blocks", "group"),
        P("blocks", "group"),
    )
    return jax.shard_map(
        on_device,
        mesh=mesh,
        in_specs=placed,
        out_specs=(P(None, None, "blocks", "group"), P("blocks", "group")),
        check_vma=False,
    )
```

profile of v0, /device:TPU:32, one launch (start us, length us, event | category | flops | bytes accessed | tf_op | source)
XLA Modules:
  0.0 868.0 jit_solution(1029576631487293257)
XLA Ops:
  2.8 4.0 collective-permute-start
  6.8 1.9 collective-permute-start.1
  10.8 5.9 collective-permute-done.1
  17.6 4.3 collective-permute-start.3
  24.3 4.7 collective-permute-done.2
  32.2 2.3 fusion.8
  34.6 1.9 collective-permute-start.4
  36.6 2.4 collective-permute-start.5
  39.0 5.8 collective-permute-done.5
  46.2 4.9 collective-permute-start.7
  52.6 1.9 collective-permute-start.8
  54.5 2.4 collective-permute-start.9
  56.9 5.8 collective-permute-done.9
  64.1 6.1 collective-permute-start.11
  72.3 124.7 %all-reduce = (f32[]{:T(128)}, f32[]{:T(128)}) all-reduce(f32[]{:T(128)} %get-tuple-element.5, f32[]{:T(128)} %get-tuple-element.4), channel_id=1, replica_groups=mesh['blocks'=64,'group'=12] {'blocks'}, use_global_device_ids=true, to_apply=%region_2.3 | all-reduce | flops 2 | bytes 16 | tf_op jit(solution)/shard_map/psum | solution.py:82
  196.9 33.8 %all-reduce.1 = (f32[]{:T(128)}, f32[]{:T(128)}) all-reduce(f32[]{:T(128)} %get-tuple-element.6, f32[]{:T(128)} %get-tuple-element.7), channel_id=1, replica_groups=mesh['blocks'=64,'group'=12] {'group'}, use_global_device_ids=true, to_apply=%region_3.4 | all-reduce | flops 2 | bytes 16 | tf_op jit(solution)/shard_map/psum | solution.py:83
  232.7 124.7 %psum.88 = f32[]{:T(128)} all-reduce(f32[]{:T(128)} %get-tuple-element.12), channel_id=1, replica_groups=mesh['blocks'=64,'group'=12] {'blocks'}, use_global_device_ids=true, to_apply=%region_8.9 | all-reduce | flops 1 | bytes 8 | tf_op jit(solution)/shard_map/psum | solution.py:82
  357.4 22.4 %psum.89 = f32[]{:T(128)} all-reduce(f32[]{:T(128)} %psum.88), channel_id=1, replica_groups=mesh['blocks'=64,'group'=12] {'group'}, use_global_device_ids=true, to_apply=%region_9.10 | all-reduce | flops 1 | bytes 8 | tf_op jit(solution)/shard_map/psum | solution.py:83
  381.2 1.9 collective-permute-start.12
  383.1 2.4 collective-permute-start.13
  385.6 5.8 collective-permute-done.13
  392.7 4.5 collective-permute-start.15
  399.3 124.7 %psum.90 = f32[]{:T(128)} all-reduce(f32[]{:T(128)} %get-tuple-element.10), channel_id=1, replica_groups=mesh['blocks'=64,'group'=12] {'blocks'}, use_global_device_ids=true, to_apply=%region_11.12 | all-reduce | flops 1 | bytes 8 | tf_op jit(solution)/shard_map/psum | solution.py:82
  524.0 23.5 %psum.91 = f32[]{:T(128)} all-reduce(f32[]{:T(128)} %psum.90), channel_id=1, replica_groups=mesh['blocks'=64,'group'=12] {'group'}, use_global_device_ids=true, to_apply=%region_12.13 | all-reduce | flops 1 | bytes 8 | tf_op jit(solution)/shard_map/psum | solution.py:83
  549.4 124.7 %psum.92 = f32[]{:T(128)} all-reduce(f32[]{:T(128)} %multiply_reduce_fusion), channel_id=1, replica_groups=mesh['blocks'=64,'group'=12] {'blocks'}, use_global_device_ids=true, to_apply=%region_14.15 | all-reduce | flops 1 | bytes 8 | tf_op jit(solution)/shard_map/psum | solution.py:82
  674.1 23.3 %psum.93 = f32[]{:T(128)} all-reduce(f32[]{:T(128)} %psum.92), channel_id=1, replica_groups=mesh['blocks'=64,'group'=12] {'group'}, use_global_device_ids=true, to_apply=%region_15.16 | all-reduce | flops 1 | bytes 8 | tf_op jit(solution)/shard_map/psum | solution.py:83
  698.8 1.9 collective-permute-start.16
  700.7 2.4 collective-permute-start.17
  703.2 5.8 collective-permute-done.17
  710.3 4.5 collective-permute-start.19
  716.9 124.7 %psum.94 = f32[]{:T(128)} all-reduce(f32[]{:T(128)} %fusion.22), channel_id=1, replica_groups=mesh['blocks'=64,'group'=12] {'blocks'}, use_global_device_ids=true, to_apply=%region_17.18 | all-reduce | flops 1 | bytes 8 | tf_op jit(solution)/shard_map/psum | solution.py:82
  842.5 23.5 %psum.95 = f32[]{:T(128)} all-reduce(f32[]{:T(128)} %psum.94), channel_id=1, replica_groups=mesh['blocks'=64,'group'=12] {'group'}, use_global_device_ids=true, to_apply=%region_18.19 | all-reduce | flops 1 | bytes 8 | tf_op jit(solution)/shard_map/psum | solution.py:83
  (83 shorter events, 26.4 us)
Async XLA Ops:
  2.8 8.0 collective-permute-start
  6.8 10.0 %collective-permute-start.1 = (f32[36,4,2,128]{3,0,2,1:T(8,128)S(1)}, f32[36,4,2,128]{3,0,2,1:T(8,128)S(1)}, u32[]{:S(2)}, u32[]{:S(2)}) collective-permute-start(f32[36,4,2,128]{3,0,2,1:T(8,128)S(1)} %get-tuple-element.25), channel_id=1, source_target_pairs={{0,12},{12,24},{24,36},{36,48},{48,60},{60,72},{72,84},{84,96},{96... | collective-permute-start | bytes 442376 | tf_op jit(solution)/shard_map/ppermute | solution.py:23
  16.7 13.6 %copy-start.2 = (f32[36,4,2,128]{3,0,2,1:T(8,128)}, f32[36,4,2,128]{3,0,2,1:T(8,128)S(1)}, u32[]{:S(2)}) copy-start(f32[36,4,2,128]{3,0,2,1:T(8,128)S(1)} %collective-permute-done.1) | copy-start | bytes 442372
  17.6 6.2 collective-permute-start.3
  22.5 6.5 collective-permute-start.2
  30.3 1.8 copy-start
  30.3 1.8 copy-start.1
  30.3 1.8 copy-start.3
  30.3 1.8 copy-start.4
  30.3 1.8 copy-start.5
  30.3 1.8 copy-start.6
  32.2 20.3 %copy-start.7 = (s32[8,128]{1,0:T(8,128)S(1)}, s32[8,128]{1,0:T(8,128)}, u32[]{:S(2)}) copy-start(s32[8,128]{1,0:T(8,128)} %param.7) | copy-start | bytes 12292
  32.2 20.3 %copy-start.8 = (f32[8,128]{1,0:T(8,128)S(1)}, f32[8,128]{1,0:T(8,128)}, u32[]{:S(2)}) copy-start(f32[8,128]{1,0:T(8,128)} %param.6) | copy-start | bytes 12292
  32.2 20.3 %copy-start.9 = (f32[8,128]{1,0:T(8,128)S(1)}, f32[8,128]{1,0:T(8,128)}, u32[]{:S(2)}) copy-start(f32[8,128]{1,0:T(8,128)} %param.5) | copy-start | bytes 12292
  34.6 4.3 collective-permute-start.4
  36.6 8.2 collective-permute-start.5
  44.9 6.2 collective-permute-start.6
  46.2 6.3 collective-permute-start.7
  52.6 4.3 collective-permute-start.8
  54.5 8.2 collective-permute-start.9
  62.8 7.4 collective-permute-start.10
  64.1 7.5 collective-permute-start.11
  381.2 4.3 collective-permute-start.12
  383.1 8.2 collective-permute-start.13
  391.4 5.8 collective-permute-start.14
  392.7 5.9 collective-permute-start.15
  698.8 4.3 collective-permute-start.16
  700.7 8.2 collective-permute-start.17
  709.0 5.8 collective-permute-start.18
  710.3 5.9 collective-permute-start.19
where the time goes:
time: 869 us; the launch traced here: 868 us
  blocking collectives  750 us (86%)
  starting transfers between devices  54 us (6%)
  waiting for transfers between devices  39.2 us (5%)
  other arithmetic  12.1 us (1%)
    psum x5, blocking collectives, global_total(): part_sum = lax.psum(value, 'blocks')  623 us
    psum x5, blocking collectives, global_total(): return lax.psum(part_sum, 'group')  127 us
    ppermute x10, starting transfers between devices, padded_2(): before = lax.ppermute(last, axis, up)  35.9 us
    ppermute x10, waiting for transfers between devices, padded_2(): before = lax.ppermute(last, axis, up)  34.5 us
    ppermute x10, starting transfers between devices, padded_2(): after = lax.ppermute(initial, axis, down)  18.1 us
  transfers between devices with their start and end apart: 20, of which 10 were waited for; matrix products, arithmetic and copies ran while one was open for 0% of the time, Pallas kernels for 0%

commit v1 on v0

v1 whole, which is shorter than its diff:
```python
import functools

import jax
import jax.numpy as jnp
from jax import lax
from jax.experimental import pallas as pl
from jax.experimental.pallas import tpu as pltpu
from jax.sharding import PartitionSpec as P

MESH = pl.DeviceIdType.MESH

time_step = 0.25
hyper_visc = 0.025
mixing = 0.2
gravity = 4.0
rotation = 0.2

SHIFT = 4.5
SCALE = 4.0
LOW, HIGH = 0.05, 9.0

GROUP_LEVELS = 6
NEAR = ((-1, 0), (1, 0), (0, -1), (0, 1), (-1, -1), (-1, 1), (1, -1), (1, 1))
OPPOSITE = (1, 0, 3, 2, 7, 6, 5, 4)
UP, DOWN, LEFT, RIGHT, UP_LEFT, UP_RIGHT, DOWN_LEFT, DOWN_RIGHT = range(8)


def roll(x, shift, axis):
    return pltpu.roll(x, shift % x.shape[axis], axis)


def kernel(
    n_blocks, n_group, inner,
    ocean, height, damping, land,
    out, surface,
    ext, sea_int, geo, geo_near, sea_ext, packed, packed_near, corner_near, halo,
    stepped, transport, transport_near, sums, sum_rows,
    load_sems, out_sems, send_sems, near_sems, sum_sems,
):
    levels = ocean.shape[0]
    groups = levels // GROUP_LEVELS
    block = lax.axis_index("blocks")
    part = lax.axis_index("group")
    outer = n_blocks // inner

    def near(n):
        db, dg = NEAR[n]
        return (lax.rem(block + (n_blocks + db), n_blocks), lax.rem(part + (n_group + dg), n_group))

    base = (block // inner) * inner
    phases = []
    phases.append([(base + lax.rem(block - base + s, inner), part) for s in range(1, inner)])
    phases.append([(lax.rem(block + s * inner, n_blocks), part) for s in range(1, outer)])
    phases.append([(block, lax.rem(part + s, n_group)) for s in range(1, n_group)])

    loads = [
        pltpu.make_async_copy(land, sea_int, load_sems.at[0]),
        pltpu.make_async_copy(damping, geo.at[1], load_sems.at[1]),
        pltpu.make_async_copy(height, geo.at[2], load_sems.at[2]),
        pltpu.make_async_copy(ocean, ext.at[1 : levels + 1, :, 8:16, :], load_sems.at[3]),
        pltpu.make_async_copy(ocean.at[0], ext.at[0, :, 8:16, :], load_sems.at[4]),
        pltpu.make_async_copy(ocean.at[levels - 1], ext.at[levels + 1, :, 8:16, :], load_sems.at[5]),
    ]
    for load in loads:
        load.start()

    barrier = pltpu.get_barrier_semaphore()
    partners = [near(n) for n in range(8)] + [p for phase in phases for p in phase]
    for partner in partners:
        pl.semaphore_signal(barrier, inc=1, device_id=partner, device_id_type=MESH)

    row = lax.broadcasted_iota(jnp.int32, (8, 128), 0)
    lane = lax.broadcasted_iota(jnp.int32, (8, 128), 1)
    first_row, last_row = row == 0, row == 7
    first_lane, last_lane = lane == 0, lane == 127
    quarter = lax.rem(lane, 4)
    field_of = lane // 4

    for load in loads[:3]:
        load.wait()
    sea = sea_int[...].astype(jnp.float32)
    geo[0] = sea
    for load in loads[3:]:
        load.wait()

    @pl.loop(0, groups)
    def _(group):
        held = jnp.zeros((8, 128), jnp.float32)
        for i in range(4 * GROUP_LEVELS):
            field = ext[group * GROUP_LEVELS + (i // 4 + 1), i % 4, 8:16, :]
            held = jnp.where(field_of == i, roll(field, 2 + 4 * i, 1), held)
        tiled = jnp.zeros((8, 128), jnp.float32)
        packed[group] = held * packed_sea(sea, quarter, tiled)

    pl.semaphore_wait(barrier, len(partners))

    sends = []

    def send(source, target, n, sem):
        copy = pltpu.make_async_remote_copy(
            src_ref=source, dst_ref=target, send_sem=send_sems.at[len(sends)], recv_sem=near_sems.at[sem],
            device_id=near(n), device_id_type=MESH,
        )
        copy.start()
        sends.append(copy)
        return copy

    rows = [
        send(ocean.at[:, :, 0:2, :], ext.at[1 : levels + 1, :, 16:18, :], UP, 0),
        send(ocean.at[:, :, 6:8, :], ext.at[1 : levels + 1, :, 6:8, :], DOWN, 1),
    ]
    shapes = [send(geo, geo_near.at[OPPOSITE[n]], n, 2 + n) for n in range(8)]
    sides = [send(packed, packed_near.at[OPPOSITE[n] - 2], n, 8 + n) for n in (LEFT, RIGHT)]
    corners = [
        send(packed.at[:, 0:1, :], corner_near.at[OPPOSITE[n] - 4, :, 0:1, :], n, 8 + n) for n in (UP_LEFT, UP_RIGHT)
    ] + [
        send(packed.at[:, 7:8, :], corner_near.at[OPPOSITE[n] - 4, :, 0:1, :], n, 8 + n) for n in (DOWN_LEFT, DOWN_RIGHT)
    ]

    def flag(condition):
        return jnp.where(condition, jnp.float32(1.0), jnp.float32(0.0))

    has_up, has_down = flag(block > 0), flag(block < n_blocks - 1)
    has_left, has_right = flag(part > 0), flag(part < n_group - 1)
    exists = (
        has_up, has_down, has_left, has_right,
        has_up * has_left, has_up * has_right, has_down * has_left, has_down * has_right,
    )

    for copy in shapes + sides + corners:
        copy.wait_recv()

    sea_ext[0:8, :] = geo_near[UP, 0] * has_up
    sea_ext[8:16, :] = sea
    sea_ext[16:24, :] = geo_near[DOWN, 0] * has_down
    sea_n2, sea_n1 = sea_ext[6:14, :], sea_ext[7:15, :]
    sea_s1, sea_s2 = sea_ext[9:17, :], sea_ext[10:18, :]

    @pl.loop(0, groups)
    def _(group):
        own = packed[group]
        left = packed_near[0, group] * has_left
        right = packed_near[1, group] * has_right
        up_left = jnp.broadcast_to(corner_near[0, group, 0:1, :] * exists[UP_LEFT], (8, 128))
        up_right = jnp.broadcast_to(corner_near[1, group, 0:1, :] * exists[UP_RIGHT], (8, 128))
        down_left = jnp.broadcast_to(corner_near[2, group, 0:1, :] * exists[DOWN_LEFT], (8, 128))
        down_right = jnp.broadcast_to(corner_near[3, group, 0:1, :] * exists[DOWN_RIGHT], (8, 128))
        left_rows = jnp.where(first_row, up_left, roll(left, 1, 0)) + jnp.where(last_row, down_left, roll(left, -1, 0))
        right_rows = jnp.where(first_row, up_right, roll(right, 1, 0)) + jnp.where(
            last_row, down_right, roll(right, -1, 0)
        )
        at_left = (2.0 * left_rows + roll(left, 1, 1) + roll(own, -1, 1) - 4.0 * left) * has_left
        at_right = (2.0 * right_rows + roll(right, -1, 1) + roll(own, 1, 1) - 4.0 * right) * has_right
        halo[group] = jnp.where(
            quarter == 0,
            roll(right, -2, 1),
            jnp.where(quarter == 1, left, jnp.where(quarter == 2, at_right, roll(at_left, 2, 1))),
        )

    column = (part * 128 + lane).astype(jnp.float32)
    coriolis = (rotation * time_step) * (2.0 * (column + 0.5) / (128 * n_group) - 1.0)
    middle = 2.0 - jnp.where(first_row, 1.0 - has_up, 0.0) - jnp.where(last_row, 1.0 - has_down, 0.0)

    for copy in rows:
        copy.wait_recv()

    def center(level, c):
        return ext[level, c, 8:16, :] * sea

    def step(group, total):
        total_east, total_north = total
        edges = halo[group]
        for l in range(GROUP_LEVELS):
            level = group * GROUP_LEVELS + (l + 1)
            now = [center(level, c) for c in range(4)]
            u, v = now[2], now[3]
            east, north = (0.5 * time_step) * u, (0.5 * time_step) * v
            for c in range(4):
                i = 4 * l + c
                g = now[c]
                n1, s1 = ext[level, c, 7:15, :] * sea_n1, ext[level, c, 9:17, :] * sea_s1
                n2, s2 = ext[level, c, 6:14, :] * sea_n2, ext[level, c, 10:18, :] * sea_s2
                edge = roll(edges, -(4 * i + 1), 1)
                edge_twice = roll(edges, -(4 * i + 3), 1)
                west = jnp.where(first_lane, edge, roll(g, 1, 1))
                east_of = jnp.where(last_lane, edge, roll(g, -1, 1))
                twice = 2.0 * (n1 + s1) + (west + east_of) - 4.0 * g
                biharm = (
                    (n2 + s2)
                    + middle * g
                    - 4.0 * twice
                    + jnp.where(first_lane, edge_twice, roll(twice, 1, 1))
                    + jnp.where(last_lane, edge_twice, roll(twice, -1, 1))
                )
                advect = east * (s1 - n1) + north * (east_of - west)
                vertical = center(level - 1, c) + center(level + 1, c) - 2.0 * g
                new = g - advect - hyper_visc * biharm + mixing * vertical
                if c == 2:
                    new = new + coriolis * v
                elif c == 3:
                    new = new - coriolis * u
                new = new * sea
                stepped[group * GROUP_LEVELS + l, c] = new
                if c == 2:
                    total_east = total_east + new
                elif c == 3:
                    total_north = total_north + new
        return total_east, total_north

    zero = jnp.zeros((8, 128), jnp.float32)
    total_east, total_north = lax.fori_loop(0, groups, step, (zero, zero))
    transport[0] = total_east / levels
    transport[1] = total_north / levels

    beside = [send(transport, transport_near.at[OPPOSITE[n]], n, 16 + n) for n in range(8)]
    stores = [
        pltpu.make_async_copy(
            stepped.at[k * GROUP_LEVELS : (k + 1) * GROUP_LEVELS],
            out.at[k * GROUP_LEVELS : (k + 1) * GROUP_LEVELS],
            out_sems.at[k],
        )
        for k in range(groups)
    ]
    for store in stores:
        store.start()

    def around(own, others):
        low, west_half = row < 4, lane < 64
        side = jnp.where(west_half, others[RIGHT], others[LEFT])
        over = jnp.where(low, others[DOWN], others[UP])
        corner = jnp.where(
            low,
            jnp.where(west_half, others[DOWN_RIGHT], others[DOWN_LEFT]),
            jnp.where(west_half, others[UP_RIGHT], others[UP_LEFT]),
        )
        return jnp.concatenate(
            [jnp.concatenate([own, side], axis=1), jnp.concatenate([over, corner], axis=1)], axis=0
        )

    sea_near = [geo_near[n, 0] * exists[n] for n in range(8)]
    sea_all = around(sea, sea_near)
    damping_all = around(geo[1], [geo_near[n, 1] for n in range(8)])
    forced = sea_all * damping_all * around(geo[2], [geo_near[n, 2] for n in range(8)])
    own_part = sea_all * ((4.0 - SHIFT + damping_all) * (1.0 / SCALE))
    beside_part = sea_all * (1.0 / SCALE)

    for copy in beside:
        copy.wait_recv()
    east_all = sea_all * around(transport[0], [transport_near[n, 0] for n in range(8)])
    north_all = sea_all * around(transport[1], [transport_near[n, 1] for n in range(8)])
    divergence = 0.5 * (roll(east_all, -1, 0) - roll(east_all, 1, 0) + roll(north_all, -1, 1) - roll(north_all, 1, 1))
    v0 = forced - (gravity * sea_all) * divergence

    def apply(s):
        return own_part * s - beside_part * (roll(s, -1, 0) + roll(s, 1, 0) + roll(s, -1, 1) + roll(s, 1, 1))

    v1 = apply(v0)
    v2 = apply(v1)
    v3 = apply(v2)
    v0, v1, v2, v3 = (v[0:8, 0:128] for v in (v0, v1, v2, v3))

    moments = (v0 * v0, v0 * v1, v1 * v1, v1 * v2, v2 * v2, v2 * v3)
    stacked = zero
    for m, moment in enumerate(moments):
        stacked = jnp.where(row == m, jnp.sum(moment, axis=0, keepdims=True), stacked)
    stacked = jnp.sum(stacked, axis=1, keepdims=True)
    partial = jnp.sum(jnp.where(lane == row, stacked, 0.0), axis=0, keepdims=True)

    at = 0
    for number, phase in enumerate(phases):
        count = len(phase)
        if count == 0:
            continue
        size = sum_rows.shape[1]
        sums[number, 0:1, :] = partial
        sum_rows[number, count:size, :] = jnp.zeros((size - count, 128), jnp.float32)
        copies = []
        for s, partner in enumerate(phase):
            copy = pltpu.make_async_remote_copy(
                src_ref=sums.at[number, 0:1, :], dst_ref=sum_rows.at[number, s : s + 1, :],
                send_sem=send_sems.at[len(sends)], recv_sem=sum_sems.at[at],
                device_id=partner, device_id_type=MESH,
            )
            copy.start()
            copies.append(copy)
            sends.append(copy)
            at += 1
        for copy in copies:
            copy.wait_recv()
        partial = partial + jnp.sum(sum_rows[number], axis=0, keepdims=True)

    spread = jnp.broadcast_to(partial, (8, 128))
    mu = [jnp.sum(jnp.where(lane == m, spread, 0.0), axis=1, keepdims=True) for m in range(6)]
    c0, c1, c2 = coefficients(mu)
    surface[...] = c0 * v0 + c1 * v1 + c2 * v2

    for copy in sends:
        copy.wait_send()
    for store in stores:
        store.wait()


def packed_sea(sea, quarter, held):
    lane = lax.broadcasted_iota(jnp.int32, (8, 128), 1)
    held = jnp.where(lane < 4, roll(sea, 2, 1), held)
    for shift in (4, 8, 16, 32, 64):
        held = held + roll(held, shift, 1)
    return held


def coefficients(mu):
    def inner(p, q, offset=0):
        total = None
        by_power = {}
        for i, a in enumerate(p):
            for j, b in enumerate(q):
                term = a * b
                by_power[i + j] = term if i + j not in by_power else by_power[i + j] + term
        for power, weight in by_power.items():
            term = weight * mu[power + offset]
            total = term if total is None else total + term
        return total

    def alpha_of(rr, d):
        image = SHIFT * inner(d, d) + SCALE * inner(d, d, 1)
        return jnp.clip(rr / image, 1.0 / HIGH, 1.0 / LOW)

    one = jnp.ones_like(mu[0])
    r, d = [one], [one]
    rr = mu[0]
    x = []
    for iteration in range(3):
        alpha = alpha_of(rr, d)
        x = [alpha * a + (x[i] if i < len(x) else 0.0) for i, a in enumerate(d)]
        if iteration == 2:
            break
        image = [SHIFT * (d[i] if i < len(d) else 0.0) + (SCALE * d[i - 1] if i > 0 else 0.0) for i in range(len(d) + 1)]
        r = [(r[i] if i < len(r) else 0.0) - alpha * image[i] for i in range(len(image))]
        new = jnp.maximum(inner(r, r), 0.0)
        beta = jnp.clip(new / rr, 0.0, HIGH / LOW)
        d = [r[i] + (beta * d[i] if i < len(d) else 0.0) for i in range(len(r))]
        rr = new
    return x


def on_device(n_blocks, n_group, inner, ocean_state, surface_height, surface_damping, land_mask):
    levels = ocean_state.shape[0]
    groups = levels // GROUP_LEVELS
    f32 = jnp.float32
    any_space = pl.BlockSpec(memory_space=pl.ANY)
    n_sums = (inner - 1) + (n_blocks // inner - 1) + (n_group - 1)
    dma = pltpu.SemaphoreType.DMA
    return pl.pallas_call(
        functools.partial(kernel, n_blocks, n_group, inner),
        out_shape=(
            jax.ShapeDtypeStruct(ocean_state.shape, f32),
            jax.ShapeDtypeStruct(surface_height.shape, f32),
        ),
        in_specs=[any_space] * 4,
        out_specs=(any_space, pl.BlockSpec(memory_space=pltpu.VMEM)),
        scratch_shapes=[
            pltpu.VMEM((levels + 2, 4, 24, 128), f32),
            pltpu.VMEM((8, 128), jnp.int32),
            pltpu.VMEM((3, 8, 128), f32),
            pltpu.VMEM((8, 3, 8, 128), f32),
            pltpu.VMEM((24, 128), f32),
            pltpu.VMEM((groups, 8, 128), f32),
            pltpu.VMEM((2, groups, 8, 128), f32),
            pltpu.VMEM((4, groups, 8, 128), f32),
            pltpu.VMEM((groups, 8, 128), f32),
            pltpu.VMEM((levels, 4, 8, 128), f32),
            pltpu.VMEM((2, 8, 128), f32),
            pltpu.VMEM((8, 2, 8, 128), f32),
            pltpu.VMEM((3, 8, 128), f32),
            pltpu.VMEM((3, 16, 128), f32),
            dma((6,)),
            dma((groups,)),
            dma((24 + n_sums,)),
            dma((24,)),
            dma((n_sums,)),
        ],
        compiler_params=pltpu.CompilerParams(collective_id=0, has_side_effects=True),
    )(ocean_state, surface_height, surface_damping, land_mask)


def solution(mesh):
    n_blocks, n_group = mesh.shape["blocks"], mesh.shape["group"]
    inner = 8 if n_blocks % 8 == 0 and n_blocks > 8 else max(1, n_blocks // 2)
    placed = (
        P(None, None, "blocks", "group"),
        P("blocks", "group"),
        P("blocks", "group"),
        P("blocks", "group"),
    )
    return jax.shard_map(
        functools.partial(on_device, n_blocks, n_group, inner),
        mesh=mesh,
        in_specs=placed,
        out_specs=(P(None, None, "blocks", "group"), P("blocks", "group")),
        check_vma=False,
    )
```

time: 869 us -> 50.3 us (0.06)
  the two profiles are of different devices: /device:TPU:32 before, /device:TPU:2 now
where the time goes in v1:
time: 50.3 us; the launch traced here: 50.1 us
  Pallas kernels  46.9 us (93%)
  local copies, waits for them, and re-layouts  2.51 us (5%)
  between operations  0.65 us (1%)
    pallas_call x1, Pallas kernels, on_device(): pl.pallas_call(functools.partial(kernel, n_blocks, n_group, inner), out_s...  46.9 us
    unnamed x4, local copies, waits for them, and re-layouts  2.51 us

profile of v1, /device:TPU:2, one launch (start us, length us, event | category | flops | bytes accessed | tf_op | source)
XLA Modules:
  0.0 50.1 jit_solution(11233904570622877560)
XLA Ops:
  0.6 46.9 %shard_map.59 = (f32[36,4,8,128]{3,2,1,0:T(8,128)}, f32[8,128]{1,0:T(8,128)}) custom-call(f32[36,4,8,128]{3,2,1,0:T(8,128)} %ocean.1, f32[8,128]{1,0:T(8,128)} %height.1, f32[8,128]{1,0:T(8,128)} %damping.1, s32[8,128]{1,0:T(8,128)} %land.1), custom_call_target="tpu_custom_call" | custom-call | tf_op jit(solution)/shard_map/pallas_call | solution.py:353
  47.6 0.0 copy-start
  47.6 1.9 %copy.8 = f32[36,4,8,128]{3,2,1,0:T(8,128)} copy(f32[36,4,8,128]{3,2,1,0:T(8,128)} %get-tuple-element.4) | data formatting | bytes 1179648
  49.5 0.0 copy-done
  49.5 0.6 %copy.9 = f32[8,128]{1,0:T(8,128)} copy(f32[8,128]{1,0:T(8,128)S(1)} %copy-done) | data formatting | bytes 8192
Async XLA Ops:
  47.6 1.9 %copy-start = (f32[8,128]{1,0:T(8,128)S(1)}, f32[8,128]{1,0:T(8,128)}, u32[]{:S(2)}) copy-start(f32[8,128]{1,0:T(8,128)} %get-tuple-element.5) | copy-start | bytes 12292

commit v2 on v0

v2 whole, which is shorter than its diff:
```python
import functools

import jax
import jax.numpy as jnp
from jax import lax
from jax.experimental import pallas as pl
from jax.experimental.pallas import tpu as pltpu
from jax.sharding import PartitionSpec as P

MESH = pl.DeviceIdType.MESH

time_step = 0.25
hyper_visc = 0.025
mixing = 0.2
gravity = 4.0
rotation = 0.2

LOW, HIGH = 0.05, 9.0
REACH = 1.125

GROUP_LEVELS = 6
NEAR = ((-1, 0), (1, 0), (0, -1), (0, 1), (-1, -1), (-1, 1), (1, -1), (1, 1))
OPPOSITE = (1, 0, 3, 2, 7, 6, 5, 4)
UP, DOWN, LEFT, RIGHT, UP_LEFT, UP_RIGHT, DOWN_LEFT, DOWN_RIGHT = range(8)
ROUNDS = ((1, 1), (2, 2), (1, 2))


def roll(x, shift, axis):
    return pltpu.roll(x, shift % x.shape[axis], axis)


def two_sum(a, b):
    s = a + b
    t = s - a
    return s, (a - (s - t)) + (b - t)


def quick_sum(a, b):
    s = a + b
    return s, b - (s - a)


def split(a):
    c = 4097.0 * a
    high = c - (c - a)
    return high, a - high


def two_prod(a, b):
    p = a * b
    (ah, al), (bh, bl) = split(a), split(b)
    return p, ((ah * bh - p) + ah * bl + al * bh) + al * bl


def add(a, b):
    s, e = two_sum(a[0], b[0])
    return quick_sum(s, e + (a[1] + b[1]))


def scale(a, power_of_two):
    return a[0] * power_of_two, a[1] * power_of_two


def minus(a, b):
    return add(a, (-b[0], -b[1]))


def mul(a, b):
    p, e = two_prod(a[0], b[0])
    return quick_sum(p, e + (a[0] * b[1] + a[1] * b[0]))


def div(a, b):
    first = a[0] / b[0]
    rest = minus(a, mul(b, (first, jnp.zeros_like(first))))
    return quick_sum(first, rest[0] / b[0])


def sum_rows_of(x):
    parts = [(x[i : i + 8], None) for i in range(0, x.shape[0], 8)]
    while len(parts) > 1:
        parts = [join(*parts[i : i + 2]) for i in range(0, len(parts), 2)]
    part = parts[0]
    for shift in (4, 2, 1):
        other = (roll(part[0], shift, 0), None if part[1] is None else roll(part[1], shift, 0))
        part = join(part, other)
    return part


def join(a, b=None):
    if b is None:
        return a
    s, e = two_sum(a[0], b[0])
    for low in (a[1], b[1]):
        if low is not None:
            e = e + low
    return s, e


def kernel(
    n_blocks, n_group, inner,
    ocean, height, damping, land,
    out, surface,
    own, sea_int, geo, geo_near, rows_own, rows_near, rows_fix, packed, packed_near, corner_near, packed_fix,
    sums_own, sums_near, transport, transport_near, row_out, rows_in,
    load_sems, send_sems, near_sems, sum_sems, greet_sems,
):
    levels = ocean.shape[0]
    groups = levels // GROUP_LEVELS
    block = lax.axis_index("blocks")
    part = lax.axis_index("group")
    outer = n_blocks // inner

    def near(n):
        db, dg = NEAR[n]
        return (lax.rem(block + (n_blocks + db), n_blocks), lax.rem(part + (n_group + dg), n_group))

    base = (block // inner) * inner

    def along_blocks(distance):
        return (lax.rem(block + (distance % n_blocks), n_blocks), part)

    def along_group(distance):
        return (block, lax.rem(part + (distance % n_group), n_group))

    def far_first(n):
        return sorted(range(1, n), key=lambda s: -min(s, n - s))

    phases = [[along_blocks(s) for s in far_first(n_blocks)], [along_group(s) for s in far_first(n_group)]]
    rounds = []
    for rows_off, group_off in ROUNDS:
        targets = []
        if rows_off % outer:
            targets += [along_blocks(rows_off * inner), along_blocks(-rows_off * inner)]
        if group_off % n_group:
            targets += [along_group(group_off), along_group(-group_off)]
        rounds.append(targets)

    loads = [
        pltpu.make_async_copy(land, sea_int, load_sems.at[0]),
        pltpu.make_async_copy(damping, geo.at[1], load_sems.at[1]),
        pltpu.make_async_copy(height, geo.at[2], load_sems.at[2]),
        pltpu.make_async_copy(ocean, own.at[1 : levels + 1], load_sems.at[3]),
        pltpu.make_async_copy(ocean.at[0], own.at[0], load_sems.at[4]),
        pltpu.make_async_copy(ocean.at[levels - 1], own.at[levels + 1], load_sems.at[5]),
        pltpu.make_async_copy(ocean.at[:, 2, 0, :], rows_own.at[0], load_sems.at[6]),
        pltpu.make_async_copy(ocean.at[:, 2, 7, :], rows_own.at[1], load_sems.at[7]),
    ]

    barrier = pltpu.get_barrier_semaphore()
    partners = (
        [near(n) for n in range(8)]
        + [(base + lax.rem(block - base + s, inner), part) for s in range(1, inner)]
        + ([along_blocks(inner), along_blocks(-inner)] if outer > 1 else [])
    )
    for partner in partners:
        pl.semaphore_signal(barrier, inc=1, device_id=partner, device_id_type=MESH)
    for load in loads:
        load.start()

    row = lax.broadcasted_iota(jnp.int32, (8, 128), 0)
    lane = lax.broadcasted_iota(jnp.int32, (8, 128), 1)
    first_row, last_row = row == 0, row == 7
    first_lane, last_lane = lane == 0, lane == 127
    quarter = lax.rem(lane, 4)
    field_of = lane // 4
    zero = jnp.zeros((8, 128), jnp.float32)

    def flag(condition):
        return jnp.where(condition, jnp.float32(1.0), jnp.float32(0.0))

    has_up, has_down = flag(block > 0), flag(block < n_blocks - 1)
    has_left, has_right = flag(part > 0), flag(part < n_group - 1)
    exists = (
        has_up, has_down, has_left, has_right,
        has_up * has_left, has_up * has_right, has_down * has_left, has_down * has_right,
    )

    sends = []

    def send(source, target, partner, sem):
        copy = pltpu.make_async_remote_copy(
            src_ref=source, dst_ref=target, send_sem=send_sems.at[len(sends)], recv_sem=sem,
            device_id=partner, device_id_type=MESH,
        )
        copy.start()
        sends.append(copy)
        return copy

    pl.semaphore_wait(barrier, len(partners))

    def greet(n):
        for target in rounds[n]:
            pl.semaphore_signal(greet_sems.at[n], inc=1, device_id=target, device_id_type=MESH)

    def greeted(n):
        if rounds[n]:
            pl.semaphore_wait(greet_sems.at[n], len(rounds[n]))

    greet(0)

    def send_rows(c):
        copies = []
        for r in range(2):
            copies.append(send(ocean.at[:, c, r, :], rows_near.at[1, r, c], near(UP), near_sems.at[4 * c + r]))
            copies.append(
                send(ocean.at[:, c, 7 - r, :], rows_near.at[0, r, c], near(DOWN), near_sems.at[4 * c + 2 + r])
            )
        return copies

    flow_rows = send_rows(2) + send_rows(3)

    for load in loads[:3]:
        load.wait()
    sea = sea_int[...].astype(jnp.float32)
    geo[0] = sea
    at = 16
    shapes = [send(geo, geo_near.at[OPPOSITE[n]], near(n), near_sems.at[at + n]) for n in range(8)]

    sea_packed = jnp.where(lane < 4, roll(sea, 2, 1), 0.0)
    for shift in (4, 8, 16, 32, 64):
        sea_packed = sea_packed + roll(sea_packed, shift, 1)

    for load in loads[3:]:
        load.wait()

    @pl.loop(0, groups)
    def _(group):
        held = [zero, zero, zero]
        for i in range(4 * GROUP_LEVELS):
            field = own[group * GROUP_LEVELS + (i // 4 + 1), i % 4]
            held[i % 3] = jnp.where(field_of == i, roll(field, 2 + 4 * i, 1), held[i % 3])
        packed[group] = (held[0] + held[1] + held[2]) * sea_packed

    at = 24
    sides = [
        send(packed, packed_near.at[OPPOSITE[n] - 2], near(n), near_sems.at[at + n - 2]) for n in (LEFT, RIGHT)
    ]
    at = 26
    corners = []
    for n in (UP_LEFT, UP_RIGHT, DOWN_LEFT, DOWN_RIGHT):
        edge = 0 if NEAR[n][0] < 0 else 7
        corners.append(
            send(
                packed.at[:, edge : edge + 1, :],
                corner_near.at[OPPOSITE[n] - 4, :, 0:1, :],
                near(n),
                near_sems.at[at + n - 4],
            )
        )
    tracer_rows = send_rows(0) + send_rows(1)

    column = (part * 128 + lane).astype(jnp.float32)
    coriolis = (rotation * time_step) * (2.0 * (column + 0.5) / (128 * n_group) - 1.0)
    middle = 2.0 - jnp.where(first_row, 1.0 - has_up, 0.0) - jnp.where(last_row, 1.0 - has_down, 0.0)
    not_first, not_last = flag(row > 0), flag(row < 7)

    def step(level, carry):
        totals, above, now = carry
        below = tuple(own[level + 2, c] * sea for c in range(4))
        u, v = now[2], now[3]
        east, north = (0.5 * time_step) * u, (0.5 * time_step) * v
        totals = list(totals)
        for c in range(4):
            g = now[c]
            n1, s1 = not_first * roll(g, 1, 0), not_last * roll(g, -1, 0)
            n2, s2 = not_first * roll(n1, 1, 0), not_last * roll(s1, -1, 0)
            west = jnp.where(first_lane, 0.0, roll(g, 1, 1))
            east_of = jnp.where(last_lane, 0.0, roll(g, -1, 1))
            twice = 2.0 * (n1 + s1) + (west + east_of) - 4.0 * g
            biharm = (
                (n2 + s2)
                + middle * g
                - 4.0 * twice
                + jnp.where(first_lane, 0.0, roll(twice, 1, 1))
                + jnp.where(last_lane, 0.0, roll(twice, -1, 1))
            )
            advect = east * (s1 - n1) + north * (east_of - west)
            vertical = above[c] + below[c] - 2.0 * g
            new = g - advect - hyper_visc * biharm + mixing * vertical
            if c == 2:
                new = new + coriolis * v
            elif c == 3:
                new = new - coriolis * u
            new = new * sea
            out[level, c] = new
            if c >= 2:
                totals[c - 2] = totals[c - 2] + new
                totals[c] = totals[c] + g
        return tuple(totals), now, below

    top = tuple(own[0, c] * sea for c in range(4))
    now = tuple(own[1, c] * sea for c in range(4))
    totals, _, _ = lax.fori_loop(0, levels, step, ((zero, zero, zero, zero), top, now))
    sums_own[0] = totals[2]
    sums_own[1] = totals[3]
    at = 30
    shared = [send(sums_own, sums_near.at[OPPOSITE[n]], near(n), near_sems.at[at + n]) for n in range(8)]
    greeted(0)
    greet(1)

    own_flow = []
    for group in range(groups):
        flow = jnp.where(lax.rem(field_of, 4) == 3, packed[group], 0.0)
        flow = flow + roll(flow, -4, 1)
        own_flow.append((0.5 * time_step) * (flow + roll(flow, -8, 1)))

    for copy in shapes[:4] + sides + flow_rows:
        copy.wait_recv()

    sea_rows = (
        (geo_near[UP, 0, 7:8, :] * has_up, geo_near[UP, 0, 6:7, :] * has_up),
        (geo_near[DOWN, 0, 0:1, :] * has_down, geo_near[DOWN, 0, 1:2, :] * has_down),
    )
    own_rows = ((geo[0, 0:1, :], geo[0, 1:2, :]), (geo[0, 7:8, :], geo[0, 6:7, :]))
    edge_lane = lax.broadcasted_iota(jnp.int32, (levels, 128), 1)
    no_west, no_east = edge_lane == 0, edge_lane == 127

    def fix_rows(c):
        totals = []
        for side in range(2):
            outer_sign = (0.5 * time_step) if side == 0 else -(0.5 * time_step)
            a = rows_near[side, 0, c] * sea_rows[side][0]
            b = rows_near[side, 1, c] * sea_rows[side][1]
            across = jnp.where(no_west, 0.0, roll(a, 1, 1)) + jnp.where(no_east, 0.0, roll(a, -1, 1))
            nearest = (
                -hyper_visc * (b - 8.0 * a + 2.0 * across) + (outer_sign * own_rows[side][0]) * rows_own[side] * a
            ) * own_rows[side][0]
            second = (-hyper_visc * a) * own_rows[side][1]
            rows_fix[side, 0, c] = nearest
            rows_fix[side, 1, c] = second
            totals.append(jnp.sum(nearest, axis=0, keepdims=True))
            totals.append(jnp.sum(second, axis=0, keepdims=True))
        first, second, last, before_last = (jnp.broadcast_to(t, (8, 128)) for t in totals)
        return jnp.where(
            first_row,
            first,
            jnp.where(row == 1, second, jnp.where(last_row, last, jnp.where(row == 6, before_last, 0.0))),
        )

    def fix_columns(group):
        mine = packed[group]
        left = packed_near[0, group] * has_left
        right = packed_near[1, group] * has_right
        left_rows = not_first * roll(left, 1, 0) + not_last * roll(left, -1, 0)
        right_rows = not_first * roll(right, 1, 0) + not_last * roll(right, -1, 0)
        at_left = 2.0 * left_rows + roll(left, 1, 1) + has_left * roll(mine, -1, 1) - 8.0 * left
        at_right = 2.0 * right_rows + roll(right, -1, 1) + has_right * roll(mine, 1, 1) - 8.0 * right
        flow = own_flow[group]
        fixed = jnp.where(
            quarter == 0,
            -hyper_visc * roll(right, -2, 1),
            jnp.where(
                quarter == 1,
                -hyper_visc * roll(at_right, -1, 1) - flow * roll(right, -1, 1),
                jnp.where(
                    quarter == 2,
                    -hyper_visc * roll(at_left, 1, 1) + flow * roll(left, 1, 1),
                    -hyper_visc * roll(left, 2, 1),
                ),
            ),
        )
        return fixed * sea_packed

    beside_edges = (lane < 2) | (lane >= 126)
    columns_total = zero
    for group in range(groups):
        fixed = fix_columns(group)
        packed_fix[group] = fixed
        columns_total = columns_total + fixed
    gathered = columns_total
    for l in range(1, GROUP_LEVELS):
        gathered = gathered + roll(columns_total, -16 * l, 1)
    for c in (2, 3):
        at_columns = jnp.where(beside_edges, roll(gathered, -(4 * c + 2), 1), 0.0)
        transport[c - 2] = (totals[c - 2] + fix_rows(c) + at_columns) / levels

    at = 38
    beside = [send(transport, transport_near.at[OPPOSITE[n]], near(n), near_sems.at[at + n]) for n in range(8)]
    greeted(1)
    greet(2)

    for copy in shapes[4:] + corners + tracer_rows + shared:
        copy.wait_recv()

    fix_rows(0)
    fix_rows(1)

    def finish(group, carry):
        def at_corner(n):
            return jnp.broadcast_to(corner_near[n - 4, group, 0:1, :] * exists[n], (8, 128))

        left_corner = jnp.where(first_row, at_corner(UP_LEFT), jnp.where(last_row, at_corner(DOWN_LEFT), 0.0))
        right_corner = jnp.where(first_row, at_corner(UP_RIGHT), jnp.where(last_row, at_corner(DOWN_RIGHT), 0.0))
        corner = jnp.where(
            quarter == 1, roll(right_corner, -1, 1), jnp.where(quarter == 2, roll(left_corner, 1, 1), 0.0)
        )
        fixed = packed_fix[group] - (2.0 * hyper_visc) * corner * sea_packed
        for i in range(4 * GROUP_LEVELS):
            level, c = group * GROUP_LEVELS + i // 4, i % 4
            first, second, last, before_last = (
                jnp.broadcast_to(rows_fix[side, r, c, pl.ds(level, 1), :], (8, 128))
                for side in range(2)
                for r in range(2)
            )
            by_rows = jnp.where(
                first_row,
                first,
                jnp.where(row == 1, second, jnp.where(last_row, last, jnp.where(row == 6, before_last, 0.0))),
            )
            by_columns = jnp.where(beside_edges, roll(fixed, -(4 * i + 2), 1), 0.0)
            out[level, c] = out[level, c] + by_rows + by_columns
        return carry

    lax.fori_loop(0, groups, finish, 0)

    def around(mine, others):
        low, west_half = row < 4, lane < 64
        side = jnp.where(west_half, others[RIGHT], others[LEFT])
        over = jnp.where(low, others[DOWN], others[UP])
        corner = jnp.where(
            low,
            jnp.where(west_half, others[DOWN_RIGHT], others[DOWN_LEFT]),
            jnp.where(west_half, others[UP_RIGHT], others[UP_LEFT]),
        )
        return jnp.concatenate(
            [jnp.concatenate([mine, side], axis=1), jnp.concatenate([over, corner], axis=1)], axis=0
        )

    ring_row = lax.broadcasted_iota(jnp.int32, (16, 256), 0)
    ring_lane = lax.broadcasted_iota(jnp.int32, (16, 256), 1)

    def over_corners(x):
        x = jnp.where(
            (ring_row == 0) | (ring_row == 8),
            roll(x, 1, 0),
            jnp.where((ring_row == 7) | (ring_row == 15), roll(x, -1, 0), 0.0),
        )
        return jnp.where(
            (ring_lane == 0) | (ring_lane == 128),
            roll(x, 1, 1),
            jnp.where((ring_lane == 127) | (ring_lane == 255), roll(x, -1, 1), 0.0),
        )

    sea_all = around(sea, [geo_near[n, 0] * exists[n] for n in range(8)])
    damping_all = around(geo[1], [geo_near[n, 1] for n in range(8)])
    forced = sea_all * damping_all * around(geo[2], [geo_near[n, 2] for n in range(8)])
    missing = [
        ((-2.0 * hyper_visc) / levels)
        * over_corners(sea_all * around(sums_own[m], [sums_near[n, m] for n in range(8)]))
        for m in range(2)
    ]
    own_part = sea_all * ((damping_all - 0.5) * 0.25)
    own_split = split(own_part)
    beside_part = sea_all * -0.25

    for copy in beside:
        copy.wait_recv()
    east_all = sea_all * (around(transport[0], [transport_near[n, 0] for n in range(8)]) + missing[0])
    north_all = sea_all * (around(transport[1], [transport_near[n, 1] for n in range(8)]) + missing[1])
    divergence = 0.5 * (roll(east_all, -1, 0) - roll(east_all, 1, 0) + roll(north_all, -1, 1) - roll(north_all, 1, 1))
    v0 = forced - (gravity * sea_all) * divergence

    def apply(s):
        high, low = s
        up, down = (roll(high, 1, 0), low if low is None else roll(low, 1, 0)), (roll(high, -1, 0), low if low is None else roll(low, -1, 0))
        west, east = (roll(high, 1, 1), low if low is None else roll(low, 1, 1)), (roll(high, -1, 1), low if low is None else roll(low, -1, 1))
        total = join(join(up, down), join(west, east))
        high_split = split(high)
        p = own_part * high
        (ah, al), (bh, bl) = own_split, high_split
        e = ((ah * bh - p) + ah * bl + al * bh) + al * bl
        if low is not None:
            e = e + own_part * low
        return add((p, e), (beside_part * total[0], beside_part * total[1]))

    v1 = apply((v0, None))
    v2 = apply(v1)
    v3 = apply(v2)
    v0 = v0[0:8, 0:128]
    v1, v2, v3 = (tuple(x[0:8, 0:128] for x in v) for v in (v1, v2, v3))
    v0 = (v0, zero)

    high, low = zero, zero
    for m, (a, b) in enumerate(((v0, v0), (v0, v1), (v1, v1), (v1, v2), (v2, v2), (v2, v3))):
        p, e = two_prod(a[0], b[0])
        e = e + (a[0] * b[1] + a[1] * b[0])
        part_sum = (p, e)
        for shift in (4, 2, 1):
            part_sum = join(part_sum, (roll(part_sum[0], shift, 0), roll(part_sum[1], shift, 0)))
        high = jnp.where(row == m, part_sum[0], high)
        low = jnp.where(row == m, part_sum[1], low)
    total = (high, low)
    for shift in (64, 32, 16, 8, 4, 2, 1):
        total = join(total, (roll(total[0], shift, 1), roll(total[1], shift, 1)))
    value = jnp.sum(
        jnp.where(lane == row, total[0], jnp.where(lane == row + 64, total[1], 0.0)), axis=0, keepdims=True
    )

    greeted(2)
    at = 0
    for number, phase in enumerate(phases):
        count = len(phase)
        size = -(-(count + 1) // 8) * 8
        row_out[number, 0:1, :] = value
        copies = []
        for s, partner in enumerate(phase):
            copies.append(
                send(row_out.at[number, 0:1, :], rows_in.at[number, s : s + 1, :], partner, sum_sems.at[at + s])
            )
        at += count
        for copy in copies:
            copy.wait_recv()
        got = rows_in[number, 0:size, :]
        row_number = lax.broadcasted_iota(jnp.int32, (size, 128), 0)
        got = jnp.where(row_number < count, got, jnp.where(row_number == count, row_out[number, 0:1, :], 0.0))
        summed, lost = sum_rows_of(got)
        value = jnp.where(lane < 64, summed, summed + roll(lost, 64, 1))[0:1, :]

    spread = jnp.broadcast_to(value, (8, 128))

    def pick(m):
        return jnp.sum(jnp.where(lane == m, spread, 0.0), axis=1, keepdims=True)

    mu = [quick_sum(pick(m), pick(64 + m)) for m in range(6)]
    surface[...] = combine(mu, v0, v1, v2)

    for copy in sends:
        copy.wait_send()


def combine(mu, v0, v1, v2):
    a = [add(scale(add(mu[k], mu[k + 1]), 4.0), scale(mu[k], 0.5)) for k in range(5)]
    l1, l2 = div(a[1], a[0]), div(a[2], a[0])
    s11 = minus(a[2], mul(l1, a[1]))
    s12 = minus(a[3], mul(l1, a[2]))
    s22 = minus(a[4], mul(l2, a[2]))
    y1 = minus(mu[1], mul(l1, mu[0]))
    y2 = minus(mu[2], mul(l2, mu[0]))
    sound = s11[0] > 0.0
    one = jnp.ones_like(s11[0])
    none = jnp.zeros_like(s11[0])
    s11 = (jnp.where(sound, s11[0], one), jnp.where(sound, s11[1], none))
    l21 = div(s12, s11)
    inside = sound & (jnp.abs(l21[0] - l1[0]) <= REACH)
    bounded = jnp.clip(l21[0], l1[0] - REACH, l1[0] + REACH)
    l21 = (
        jnp.where(sound, jnp.where(inside, l21[0], bounded), l1[0]),
        jnp.where(sound, jnp.where(inside, l21[1], none), l1[1]),
    )
    t22 = minus(s22, mul(l21, s12))
    z2 = minus(y2, mul(l21, y1))

    def step_of(quotient):
        return jnp.clip(quotient, 1.0 / HIGH, 1.0 / LOW)

    alpha0 = step_of(mu[0][0] / a[0][0])
    alpha1 = step_of(y1[0] / (s11[0] * (-4.0 * alpha0)))
    firm = t22[0] > 0.0
    alpha2 = step_of(z2[0] / (jnp.where(firm, t22[0], one) * (16.0 * alpha0 * alpha1)))

    def wide(pair):
        return tuple(jnp.broadcast_to(x, v0[0].shape) for x in pair)

    l1, l2, l21 = wide(l1), wide(l2), wide(l21)
    p1 = minus(v1, mul(l1, v0))
    p2 = minus(v2, add(mul(l2, v0), mul(l21, p1)))
    return alpha0 * (v0[0] + alpha1 * (-4.0 * p1[0] + (16.0 * alpha2) * p2[0]))


def on_device(n_blocks, n_group, inner, ocean_state, surface_height, surface_damping, land_mask):
    levels = ocean_state.shape[0]
    groups = levels // GROUP_LEVELS
    f32 = jnp.float32
    any_space = pl.BlockSpec(memory_space=pl.ANY)
    vmem = pl.BlockSpec(memory_space=pltpu.VMEM)
    n_sums = (n_blocks - 1) + (n_group - 1)
    dma = pltpu.SemaphoreType.DMA
    return pl.pallas_call(
        functools.partial(kernel, n_blocks, n_group, inner),
        out_shape=(pltpu.VMEM(ocean_state.shape, f32), pltpu.VMEM(surface_height.shape, f32)),
        in_specs=[any_space] * 4,
        out_specs=(vmem, vmem),
        scratch_shapes=[
            pltpu.VMEM((levels + 2, 4, 8, 128), f32),
            pltpu.VMEM((8, 128), jnp.int32),
            pltpu.VMEM((3, 8, 128), f32),
            pltpu.VMEM((8, 3, 8, 128), f32),
            pltpu.VMEM((2, levels, 128), f32),
            pltpu.VMEM((2, 2, 4, levels, 128), f32),
            pltpu.VMEM((2, 2, 4, levels, 128), f32),
            pltpu.VMEM((groups, 8, 128), f32),
            pltpu.VMEM((2, groups, 8, 128), f32),
            pltpu.VMEM((4, groups, 8, 128), f32),
            pltpu.VMEM((groups, 8, 128), f32),
            pltpu.VMEM((2, 8, 128), f32),
            pltpu.VMEM((8, 2, 8, 128), f32),
            pltpu.VMEM((2, 8, 128), f32),
            pltpu.VMEM((8, 2, 8, 128), f32),
            pltpu.VMEM((2, 8, 128), f32),
            pltpu.VMEM((2, max(n_blocks, 16), 128), f32),
            dma((8,)),
            dma((46 + n_sums,)),
            dma((46,)),
            dma((n_sums,)),
            pltpu.SemaphoreType.REGULAR((len(ROUNDS),)),
        ],
        compiler_params=pltpu.CompilerParams(collective_id=0, has_side_effects=True),
    )(ocean_state, surface_height, surface_damping, land_mask)


def solution(mesh):
    n_blocks, n_group = mesh.shape["blocks"], mesh.shape["group"]
    inner = 8 if n_blocks % 8 == 0 and n_blocks > 8 else max(1, n_blocks // 2)
    placed = (
        P(None, None, "blocks", "group"),
        P("blocks", "group"),
        P("blocks", "group"),
        P("blocks", "group"),
    )
    return jax.shard_map(
        functools.partial(on_device, n_blocks, n_group, inner),
        mesh=mesh,
        in_specs=placed,
        out_specs=(P(None, None, "blocks", "group"), P("blocks", "group")),
        check_vma=False,
    )
```

time: 869 us -> 46.5 us (0.05)
  the two profiles are of different devices: /device:TPU:32 before, /device:TPU:1 now
where the time goes in v2:
time: 46.5 us; the launch traced here: 46.3 us
  Pallas kernels  44.2 us (95%)
  local copies, waits for them, and re-layouts  1.41 us (3%)
  between operations  0.64 us (1%)
    pallas_call x1, Pallas kernels, on_device(): pl.pallas_call(functools.partial(kernel, n_blocks, n_group, inner), out_s...  44.2 us
    unnamed x2, local copies, waits for them, and re-layouts  1.41 us

profile of v2, /device:TPU:1, one launch (start us, length us, event | category | flops | bytes accessed | tf_op | source)
XLA Modules:
  0.0 46.3 jit_solution(13007992343995669336)
XLA Ops:
  0.6 44.2 %shard_map.59 = (f32[36,4,8,128]{3,2,1,0:T(8,128)S(1)}, f32[8,128]{1,0:T(8,128)S(1)}) custom-call(f32[36,4,8,128]{3,2,1,0:T(8,128)} %ocean.1, f32[8,128]{1,0:T(8,128)} %height.1, f32[8,128]{1,0:T(8,128)} %damping.1, s32[8,128]{1,0:T(8,128)} %land.1), custom_call_target="tpu_custom_call" | custom-call | tf_op jit(solution)/shard_map/pallas_call | solution.py:579
  44.9 0.8 %copy.8 = f32[36,4,8,128]{3,2,1,0:T(8,128)} copy(f32[36,4,8,128]{3,2,1,0:T(8,128)S(1)} %get-tuple-element.2) | data formatting | bytes 1179648
  45.7 0.6 %copy.9 = f32[8,128]{1,0:T(8,128)} copy(f32[8,128]{1,0:T(8,128)S(1)} %get-tuple-element.3) | data formatting | bytes 8192

commit v3 on v2

--- a/solution.py
+++ b/solution.py
@@ -102,8 +102,8 @@
     ocean, height, damping, land,
     out, surface,
     own, sea_int, geo, geo_near, rows_own, rows_near, rows_fix, packed, packed_near, corner_near, packed_fix,
-    sums_own, sums_near, transport, transport_near, row_out, rows_in,
-    load_sems, send_sems, near_sems, sum_sems, greet_sems,
+    flow, flow_near, sums_own, sums_near, row_out, rows_in,
+    load_sems, send_sems, near_sems, greet_sems,
 ):
     levels = ocean.shape[0]
     groups = levels // GROUP_LEVELS
@@ -143,9 +143,14 @@
         pltpu.make_async_copy(ocean, own.at[1 : levels + 1], load_sems.at[3]),
         pltpu.make_async_copy(ocean.at[0], own.at[0], load_sems.at[4]),
         pltpu.make_async_copy(ocean.at[levels - 1], own.at[levels + 1], load_sems.at[5]),
-        pltpu.make_async_copy(ocean.at[:, 2, 0, :], rows_own.at[0], load_sems.at[6]),
-        pltpu.make_async_copy(ocean.at[:, 2, 7, :], rows_own.at[1], load_sems.at[7]),
     ]
+    for side in range(2):
+        for c in range(2):
+            loads.append(
+                pltpu.make_async_copy(
+                    ocean.at[:, c + 2, 7 * side, :], rows_own.at[side, c], load_sems.at[6 + 2 * side + c]
+                )
+            )
 
     barrier = pltpu.get_barrier_semaphore()
     partners = (
@@ -178,9 +183,9 @@
 
     sends = []
 
-    def send(source, target, partner, sem):
+    def send(source, target, partner):
         copy = pltpu.make_async_remote_copy(
-            src_ref=source, dst_ref=target, send_sem=send_sems.at[len(sends)], recv_sem=sem,
+            src_ref=source, dst_ref=target, send_sem=send_sems.at[len(sends)], recv_sem=near_sems.at[len(sends)],
             device_id=partner, device_id_type=MESH,
         )
         copy.start()
@@ -199,30 +204,57 @@
 
     greet(0)
 
-    def send_rows(c):
-        copies = []
-        for r in range(2):
-            copies.append(send(ocean.at[:, c, r, :], rows_near.at[1, r, c], near(UP), near_sems.at[4 * c + r]))
-            copies.append(
-                send(ocean.at[:, c, 7 - r, :], rows_near.at[0, r, c], near(DOWN), near_sems.at[4 * c + 2 + r])
-            )
-        return copies
-
-    flow_rows = send_rows(2) + send_rows(3)
+    def send_rows(c, r):
+        return [
+            send(ocean.at[:, c, r, :], rows_near.at[1, r, c], near(UP)),
+            send(ocean.at[:, c, 7 - r, :], rows_near.at[0, r, c], near(DOWN)),
+        ]
+
+    flow_rows = send_rows(2, 0) + send_rows(3, 0)
 
     for load in loads[:3]:
         load.wait()
     sea = sea_int[...].astype(jnp.float32)
     geo[0] = sea
-    at = 16
-    shapes = [send(geo, geo_near.at[OPPOSITE[n]], near(n), near_sems.at[at + n]) for n in range(8)]
+    shapes = [send(geo, geo_near.at[OPPOSITE[n]], near(n)) for n in range(8)]
+
+    for load in loads[3:]:
+        load.wait()
+
+    eighth = lax.rem(lane, 8)
+    sea_flow = jnp.where(lane < 8, roll(sea, 4, 1), 0.0)
+    for shift in (8, 16, 32, 64):
+        sea_flow = sea_flow + roll(sea_flow, shift, 1)
+    for group in range(groups):
+        held = [zero, zero, zero, zero]
+        for i in range(2 * GROUP_LEVELS):
+            field = own[group * GROUP_LEVELS + (i // 2 + 1), 2 + i % 2]
+            held[i % 4] = jnp.where(lane // 8 == i, roll(field, 4 + 8 * i, 1), held[i % 4])
+        flow[group] = ((held[0] + held[1]) + (held[2] + held[3])) * sea_flow
+    flows = []
+    for n in range(8):
+        rows = {-1: pl.ds(0, 4), 0: pl.ds(0, 8), 1: pl.ds(4, 4)}[NEAR[n][0]]
+        flows.append(send(flow.at[:, rows, :], flow_near.at[OPPOSITE[n], :, rows, :], near(n)))
+
+    not_first, not_last = flag(row > 0), flag(row < 7)
+
+    def advection(level, carry):
+        u, v = own[level + 1, 2] * sea, own[level + 1, 3] * sea
+        east, north = (0.5 * time_step) * u, (0.5 * time_step) * v
+        terms = []
+        for g in (u, v):
+            along = not_last * roll(g, -1, 0) - not_first * roll(g, 1, 0)
+            across = jnp.where(last_lane, 0.0, roll(g, -1, 1)) - jnp.where(first_lane, 0.0, roll(g, 1, 1))
+            terms.append(east * along + north * across)
+        return carry[0] + u, carry[1] + v, carry[2] + terms[0], carry[3] + terms[1]
+
+    for n, total in enumerate(lax.fori_loop(0, levels, advection, (zero, zero, zero, zero), unroll=4)):
+        sums_own[n] = total
+    shared = [send(sums_own, sums_near.at[OPPOSITE[n]], near(n)) for n in range(8)]
 
     sea_packed = jnp.where(lane < 4, roll(sea, 2, 1), 0.0)
     for shift in (4, 8, 16, 32, 64):
         sea_packed = sea_packed + roll(sea_packed, shift, 1)
-
-    for load in loads[3:]:
-        load.wait()
 
     @pl.loop(0, groups)
     def _(group):
@@ -232,35 +264,27 @@
             held[i % 3] = jnp.where(field_of == i, roll(field, 2 + 4 * i, 1), held[i % 3])
         packed[group] = (held[0] + held[1] + held[2]) * sea_packed
 
-    at = 24
-    sides = [
-        send(packed, packed_near.at[OPPOSITE[n] - 2], near(n), near_sems.at[at + n - 2]) for n in (LEFT, RIGHT)
-    ]
-    at = 26
+    sides = [send(packed, packed_near.at[OPPOSITE[n] - 2], near(n)) for n in (LEFT, RIGHT)]
     corners = []
     for n in (UP_LEFT, UP_RIGHT, DOWN_LEFT, DOWN_RIGHT):
         edge = 0 if NEAR[n][0] < 0 else 7
         corners.append(
-            send(
-                packed.at[:, edge : edge + 1, :],
-                corner_near.at[OPPOSITE[n] - 4, :, 0:1, :],
-                near(n),
-                near_sems.at[at + n - 4],
-            )
-        )
-    tracer_rows = send_rows(0) + send_rows(1)
+            send(packed.at[:, edge : edge + 1, :], corner_near.at[OPPOSITE[n] - 4, :, 0:1, :], near(n))
+        )
+    other_rows = send_rows(2, 1) + send_rows(3, 1)
+    for c in (0, 1):
+        other_rows += send_rows(c, 0) + send_rows(c, 1)
+    greeted(0)
+    greet(1)
 
     column = (part * 128 + lane).astype(jnp.float32)
     coriolis = (rotation * time_step) * (2.0 * (column + 0.5) / (128 * n_group) - 1.0)
     middle = 2.0 - jnp.where(first_row, 1.0 - has_up, 0.0) - jnp.where(last_row, 1.0 - has_down, 0.0)
-    not_first, not_last = flag(row > 0), flag(row < 7)
-
     def step(level, carry):
-        totals, above, now = carry
+        above, now = carry
         below = tuple(own[level + 2, c] * sea for c in range(4))
         u, v = now[2], now[3]
         east, north = (0.5 * time_step) * u, (0.5 * time_step) * v
-        totals = list(totals)
         for c in range(4):
             g = now[c]
             n1, s1 = not_first * roll(g, 1, 0), not_last * roll(g, -1, 0)
@@ -284,135 +308,13 @@
                 new = new - coriolis * u
             new = new * sea
             out[level, c] = new
-            if c >= 2:
-                totals[c - 2] = totals[c - 2] + new
-                totals[c] = totals[c] + g
-        return tuple(totals), now, below
+        return now, below
 
     top = tuple(own[0, c] * sea for c in range(4))
     now = tuple(own[1, c] * sea for c in range(4))
-    totals, _, _ = lax.fori_loop(0, levels, step, ((zero, zero, zero, zero), top, now))
-    sums_own[0] = totals[2]
-    sums_own[1] = totals[3]
-    at = 30
-    shared = [send(sums_own, sums_near.at[OPPOSITE[n]], near(n), near_sems.at[at + n]) for n in range(8)]
-    greeted(0)
-    greet(1)
-
-    own_flow = []
-    for group in range(groups):
-        flow = jnp.where(lax.rem(field_of, 4) == 3, packed[group], 0.0)
-        flow = flow + roll(flow, -4, 1)
-        own_flow.append((0.5 * time_step) * (flow + roll(flow, -8, 1)))
-
-    for copy in shapes[:4] + sides + flow_rows:
-        copy.wait_recv()
-
-    sea_rows = (
-        (geo_near[UP, 0, 7:8, :] * has_up, geo_near[UP, 0, 6:7, :] * has_up),
-        (geo_near[DOWN, 0, 0:1, :] * has_down, geo_near[DOWN, 0, 1:2, :] * has_down),
-    )
-    own_rows = ((geo[0, 0:1, :], geo[0, 1:2, :]), (geo[0, 7:8, :], geo[0, 6:7, :]))
-    edge_lane = lax.broadcasted_iota(jnp.int32, (levels, 128), 1)
-    no_west, no_east = edge_lane == 0, edge_lane == 127
-
-    def fix_rows(c):
-        totals = []
-        for side in range(2):
-            outer_sign = (0.5 * time_step) if side == 0 else -(0.5 * time_step)
-            a = rows_near[side, 0, c] * sea_rows[side][0]
-            b = rows_near[side, 1, c] * sea_rows[side][1]
-            across = jnp.where(no_west, 0.0, roll(a, 1, 1)) + jnp.where(no_east, 0.0, roll(a, -1, 1))
-            nearest = (
-                -hyper_visc * (b - 8.0 * a + 2.0 * across) + (outer_sign * own_rows[side][0]) * rows_own[side] * a
-            ) * own_rows[side][0]
-            second = (-hyper_visc * a) * own_rows[side][1]
-            rows_fix[side, 0, c] = nearest
-            rows_fix[side, 1, c] = second
-            totals.append(jnp.sum(nearest, axis=0, keepdims=True))
-            totals.append(jnp.sum(second, axis=0, keepdims=True))
-        first, second, last, before_last = (jnp.broadcast_to(t, (8, 128)) for t in totals)
-        return jnp.where(
-            first_row,
-            first,
-            jnp.where(row == 1, second, jnp.where(last_row, last, jnp.where(row == 6, before_last, 0.0))),
-        )
-
-    def fix_columns(group):
-        mine = packed[group]
-        left = packed_near[0, group] * has_left
-        right = packed_near[1, group] * has_right
-        left_rows = not_first * roll(left, 1, 0) + not_last * roll(left, -1, 0)
-        right_rows = not_first * roll(right, 1, 0) + not_last * roll(right, -1, 0)
-        at_left = 2.0 * left_rows + roll(left, 1, 1) + has_left * roll(mine, -1, 1) - 8.0 * left
-        at_right = 2.0 * right_rows + roll(right, -1, 1) + has_right * roll(mine, 1, 1) - 8.0 * right
-        flow = own_flow[group]
-        fixed = jnp.where(
-            quarter == 0,
-            -hyper_visc * roll(right, -2, 1),
-            jnp.where(
-                quarter == 1,
-                -hyper_visc * roll(at_right, -1, 1) - flow * roll(right, -1, 1),
-                jnp.where(
-                    quarter == 2,
-                    -hyper_visc * roll(at_left, 1, 1) + flow * roll(left, 1, 1),
-                    -hyper_visc * roll(left, 2, 1),
-                ),
-            ),
-        )
-        return fixed * sea_packed
-
-    beside_edges = (lane < 2) | (lane >= 126)
-    columns_total = zero
-    for group in range(groups):
-        fixed = fix_columns(group)
-        packed_fix[group] = fixed
-        columns_total = columns_total + fixed
-    gathered = columns_total
-    for l in range(1, GROUP_LEVELS):
-        gathered = gathered + roll(columns_total, -16 * l, 1)
-    for c in (2, 3):
-        at_columns = jnp.where(beside_edges, roll(gathered, -(4 * c + 2), 1), 0.0)
-        transport[c - 2] = (totals[c - 2] + fix_rows(c) + at_columns) / levels
-
-    at = 38
-    beside = [send(transport, transport_near.at[OPPOSITE[n]], near(n), near_sems.at[at + n]) for n in range(8)]
+    lax.fori_loop(0, levels, step, (top, now))
     greeted(1)
     greet(2)
-
-    for copy in shapes[4:] + corners + tracer_rows + shared:
-        copy.wait_recv()
-
-    fix_rows(0)
-    fix_rows(1)
-
-    def finish(group, carry):
-        def at_corner(n):
-            return jnp.broadcast_to(corner_near[n - 4, group, 0:1, :] * exists[n], (8, 128))
-
-        left_corner = jnp.where(first_row, at_corner(UP_LEFT), jnp.where(last_row, at_corner(DOWN_LEFT), 0.0))
-        right_corner = jnp.where(first_row, at_corner(UP_RIGHT), jnp.where(last_row, at_corner(DOWN_RIGHT), 0.0))
-        corner = jnp.where(
-            quarter == 1, roll(right_corner, -1, 1), jnp.where(quarter == 2, roll(left_corner, 1, 1), 0.0)
-        )
-        fixed = packed_fix[group] - (2.0 * hyper_visc) * corner * sea_packed
-        for i in range(4 * GROUP_LEVELS):
-            level, c = group * GROUP_LEVELS + i // 4, i % 4
-            first, second, last, before_last = (
-                jnp.broadcast_to(rows_fix[side, r, c, pl.ds(level, 1), :], (8, 128))
-                for side in range(2)
-                for r in range(2)
-            )
-            by_rows = jnp.where(
-                first_row,
-                first,
-                jnp.where(row == 1, second, jnp.where(last_row, last, jnp.where(row == 6, before_last, 0.0))),
-            )
-            by_columns = jnp.where(beside_edges, roll(fixed, -(4 * i + 2), 1), 0.0)
-            out[level, c] = out[level, c] + by_rows + by_columns
-        return carry
-
-    lax.fori_loop(0, groups, finish, 0)
 
     def around(mine, others):
         low, west_half = row < 4, lane < 64
@@ -427,39 +329,213 @@
             [jnp.concatenate([mine, side], axis=1), jnp.concatenate([over, corner], axis=1)], axis=0
         )
 
-    ring_row = lax.broadcasted_iota(jnp.int32, (16, 256), 0)
-    ring_lane = lax.broadcasted_iota(jnp.int32, (16, 256), 1)
-
-    def over_corners(x):
-        x = jnp.where(
-            (ring_row == 0) | (ring_row == 8),
-            roll(x, 1, 0),
-            jnp.where((ring_row == 7) | (ring_row == 15), roll(x, -1, 0), 0.0),
-        )
-        return jnp.where(
-            (ring_lane == 0) | (ring_lane == 128),
-            roll(x, 1, 1),
-            jnp.where((ring_lane == 127) | (ring_lane == 255), roll(x, -1, 1), 0.0),
-        )
-
-    sea_all = around(sea, [geo_near[n, 0] * exists[n] for n in range(8)])
+    for copy in flow_rows + shapes + flows + shared:
+        copy.wait_recv()
+
+    sea_near = [geo_near[n, 0] * exists[n] for n in range(8)]
+    sea_all = around(sea, sea_near)
     damping_all = around(geo[1], [geo_near[n, 1] for n in range(8)])
     forced = sea_all * damping_all * around(geo[2], [geo_near[n, 2] for n in range(8)])
-    missing = [
-        ((-2.0 * hyper_visc) / levels)
-        * over_corners(sea_all * around(sums_own[m], [sums_near[n, m] for n in range(8)]))
-        for m in range(2)
+
+    def around_whole(mine, others):
+        west_half = lane < 64
+        blocks = [
+            [mine, jnp.where(west_half, others[RIGHT], others[LEFT])],
+            [others[DOWN], jnp.where(west_half, others[DOWN_RIGHT], others[DOWN_LEFT])],
+            [others[UP], jnp.where(west_half, others[UP_RIGHT], others[UP_LEFT])],
+        ]
+        return jnp.concatenate([jnp.concatenate(b, axis=1) for b in blocks], axis=0)
+
+    def ring_laplace(x):
+        return (roll(x, 1, 0) + roll(x, -1, 0)) + (roll(x, 1, 1) + roll(x, -1, 1)) - 4.0 * x
+
+    inside = around_whole(zero + 1.0, [zero + exists[n] for n in range(8)])
+    ring_lane = lax.broadcasted_iota(jnp.int32, (24, 256), 1)
+    ring_column = (part * 128 + jnp.where(ring_lane < 192, ring_lane, ring_lane - 256)).astype(jnp.float32)
+    ring_coriolis = (rotation * time_step) * (2.0 * (ring_column + 0.5) / (128 * n_group) - 1.0)
+    level_sums = [
+        around_whole(sums_own[m], [sums_near[n, m] * exists[n] for n in range(8)]) for m in range(2)
     ]
+    linear = []
+    for m in range(2):
+        g = level_sums[m]
+        linear.append(
+            (g - hyper_visc * ring_laplace(inside * ring_laplace(g)))
+            + (ring_coriolis if m == 0 else -ring_coriolis) * level_sums[1 - m]
+        )
+
+    flow_lane = lane // 8
+    is_east_field = lax.rem(flow_lane, 2) == 0
+    before_edge, after_edge = flag(eighth == 3), flag(eighth == 4)
+    first, last = flag(first_row), flag(last_row)
+
+    def of_u(x):
+        x = jnp.where(is_east_field, x, 0.0)
+        return x + roll(x, 8, 1)
+
+    def of_v(x):
+        x = jnp.where(is_east_field, 0.0, x)
+        return x + roll(x, -8, 1)
+
+    def across_columns(x, beside):
+        return of_v(x) * (before_edge * roll(beside, -1, 1) - after_edge * roll(beside, 1, 1))
+
+    def across_rows(x, beside):
+        return of_u(x) * (last * roll(beside, -1, 0) - first * roll(beside, 1, 0))
+
+    gathered = [zero, zero, zero, zero]
+    for group in range(groups):
+        tiles = [flow_near[n, group] * exists[n] for n in range(8)]
+        low, ends = row < 4, eighth < 4
+        mine = flow[group]
+        over = jnp.where(low, tiles[DOWN], tiles[UP])
+        side = jnp.where(ends, tiles[LEFT], tiles[RIGHT])
+        over_side = jnp.where(
+            low,
+            jnp.where(ends, tiles[DOWN_LEFT], tiles[DOWN_RIGHT]),
+            jnp.where(ends, tiles[UP_LEFT], tiles[UP_RIGHT]),
+        )
+        gathered[0] = gathered[0] + across_columns(mine, side)
+        gathered[1] = gathered[1] + (across_columns(side, mine) + across_rows(side, over_side))
+        gathered[2] = gathered[2] + across_columns(over, over_side)
+        gathered[3] = gathered[3] + (across_columns(over_side, over) + across_rows(over_side, side))
+
+    def by_component(x, edge):
+        total = x
+        for l in range(1, GROUP_LEVELS):
+            total = total + roll(x, -16 * l, 1)
+        return [jnp.where(edge, roll(total, -(8 * c + 4), 1), 0.0) for c in range(2)]
+
+    at_edge = first_lane | last_lane
+    near_edge = (lane < 4) | (lane >= 124)
+    edges = [by_component(gathered[n], at_edge if n in (0, 2) else near_edge) for n in range(4)]
+
+    def met(x, g, weight):
+        return jnp.broadcast_to(jnp.sum(x * g, axis=0, keepdims=True) * weight, (8, 128))
+
+    above_weight = geo[0, 0:1, :] * (geo_near[UP, 0, 7:8, :] * has_up)
+    below_weight = geo[0, 7:8, :] * (geo_near[DOWN, 0, 0:1, :] * has_down)
+    advected = []
+    for m in range(2):
+        up_g, down_g = rows_near[0, 0, 2 + m], rows_near[1, 0, 2 + m]
+        inner_rows = last * met(rows_own[1, 0], down_g, below_weight) - first * met(rows_own[0, 0], up_g, above_weight)
+        outer_rows = last * met(rows_near[0, 0, 2], rows_own[0, m], above_weight) - first * met(
+            rows_near[1, 0, 2], rows_own[1, m], below_weight
+        )
+        crossing = jnp.concatenate(
+            [
+                jnp.concatenate([edges[0][m] + inner_rows, edges[1][m]], axis=1),
+                jnp.concatenate([edges[2][m] + outer_rows, edges[3][m]], axis=1),
+            ],
+            axis=0,
+        )
+        advected.append(
+            around(sums_own[2 + m], [sums_near[n, 2 + m] for n in range(8)]) + (0.5 * time_step) * crossing
+        )
+
+    ring_low = lax.broadcasted_iota(jnp.int32, (8, 256), 0) < 4
+    transport = []
+    for m in range(2):
+        nearest = jnp.concatenate(
+            [linear[m][0:8], jnp.where(ring_low, linear[m][8:16], linear[m][16:24])], axis=0
+        )
+        transport.append(sea_all * ((nearest - advected[m]) / levels))
+    east_all, north_all = transport
     own_part = sea_all * ((damping_all - 0.5) * 0.25)
     own_split = split(own_part)
     beside_part = sea_all * -0.25
 
-    for copy in beside:
-        copy.wait_recv()
-    east_all = sea_all * (around(transport[0], [transport_near[n, 0] for n in range(8)]) + missing[0])
-    north_all = sea_all * (around(transport[1], [transport_near[n, 1] for n in range(8)]) + missing[1])
     divergence = 0.5 * (roll(east_all, -1, 0) - roll(east_all, 1, 0) + roll(north_all, -1, 1) - roll(north_all, 1, 1))
     v0 = forced - (gravity * sea_all) * divergence
+
+    def finish_state():
+        own_flow = []
+        for group in range(groups):
+            north = jnp.where(lax.rem(field_of, 4) == 3, packed[group], 0.0)
+            north = north + roll(north, -4, 1)
+            own_flow.append((0.5 * time_step) * (north + roll(north, -8, 1)))
+
+        for copy in sides + corners + other_rows:
+            copy.wait_recv()
+
+        sea_rows = (
+            (geo_near[UP, 0, 7:8, :] * has_up, geo_near[UP, 0, 6:7, :] * has_up),
+            (geo_near[DOWN, 0, 0:1, :] * has_down, geo_near[DOWN, 0, 1:2, :] * has_down),
+        )
+        own_rows = ((geo[0, 0:1, :], geo[0, 1:2, :]), (geo[0, 7:8, :], geo[0, 6:7, :]))
+        edge_lane = lax.broadcasted_iota(jnp.int32, (levels, 128), 1)
+        no_west, no_east = edge_lane == 0, edge_lane == 127
+
+        def fix_rows(c):
+            for side in range(2):
+                outer_sign = (0.5 * time_step) if side == 0 else -(0.5 * time_step)
+                a = rows_near[side, 0, c] * sea_rows[side][0]
+                b = rows_near[side, 1, c] * sea_rows[side][1]
+                across = jnp.where(no_west, 0.0, roll(a, 1, 1)) + jnp.where(no_east, 0.0, roll(a, -1, 1))
+                nearest = (
+                    -hyper_visc * (b - 8.0 * a + 2.0 * across) + (outer_sign * own_rows[side][0]) * rows_own[side, 0] * a
+                ) * own_rows[side][0]
+                second = (-hyper_visc * a) * own_rows[side][1]
+                rows_fix[side, 0, c] = nearest
+                rows_fix[side, 1, c] = second
+
+        def fix_columns(group):
+            mine = packed[group]
+            left = packed_near[0, group] * has_left
+            right = packed_near[1, group] * has_right
+            left_rows = not_first * roll(left, 1, 0) + not_last * roll(left, -1, 0)
+            right_rows = not_first * roll(right, 1, 0) + not_last * roll(right, -1, 0)
+            at_left = 2.0 * left_rows + roll(left, 1, 1) + has_left * roll(mine, -1, 1) - 8.0 * left
+            at_right = 2.0 * right_rows + roll(right, -1, 1) + has_right * roll(mine, 1, 1) - 8.0 * right
+            swept = own_flow[group]
+            fixed = jnp.where(
+                quarter == 0,
+                -hyper_visc * roll(right, -2, 1),
+                jnp.where(
+                    quarter == 1,
+                    -hyper_visc * roll(at_right, -1, 1) - swept * roll(right, -1, 1),
+                    jnp.where(
+                        quarter == 2,
+                        -hyper_visc * roll(at_left, 1, 1) + swept * roll(left, 1, 1),
+                        -hyper_visc * roll(left, 2, 1),
+                    ),
+                ),
+            )
+            return fixed * sea_packed
+
+        beside_edges = (lane < 2) | (lane >= 126)
+        for group in range(groups):
+            packed_fix[group] = fix_columns(group)
+        for c in range(4):
+            fix_rows(c)
+
+        def finish(group, carry):
+            def at_corner(n):
+                return jnp.broadcast_to(corner_near[n - 4, group, 0:1, :] * exists[n], (8, 128))
+
+            left_corner = jnp.where(first_row, at_corner(UP_LEFT), jnp.where(last_row, at_corner(DOWN_LEFT), 0.0))
+            right_corner = jnp.where(first_row, at_corner(UP_RIGHT), jnp.where(last_row, at_corner(DOWN_RIGHT), 0.0))
+            corner = jnp.where(
+                quarter == 1, roll(right_corner, -1, 1), jnp.where(quarter == 2, roll(left_corner, 1, 1), 0.0)
+            )
+            fixed = packed_fix[group] - (2.0 * hyper_visc) * corner * sea_packed
+            for i in range(4 * GROUP_LEVELS):
+                level, c = group * GROUP_LEVELS + i // 4, i % 4
+                first, second, last, before_last = (
+                    jnp.broadcast_to(rows_fix[side, r, c, pl.ds(level, 1), :], (8, 128))
+                    for side in range(2)
+                    for r in range(2)
+                )
+                by_rows = jnp.where(
+                    first_row,
+                    first,
+                    jnp.where(row == 1, second, jnp.where(last_row, last, jnp.where(row == 6, before_last, 0.0))),
+                )
+                by_columns = jnp.where(beside_edges, roll(fixed, -(4 * i + 2), 1), 0.0)
+                out[level, c] = out[level, c] + by_rows + by_columns
+            return carry
+
+        lax.fori_loop(0, groups, finish, 0)
 
     def apply(s):
         high, low = s
@@ -498,7 +574,6 @@
     )
 
     greeted(2)
-    at = 0
     for number, phase in enumerate(phases):
         count = len(phase)
         size = -(-(count + 1) // 8) * 8
@@ -506,9 +581,10 @@
         copies = []
         for s, partner in enumerate(phase):
             copies.append(
-                send(row_out.at[number, 0:1, :], rows_in.at[number, s : s + 1, :], partner, sum_sems.at[at + s])
+                send(row_out.at[number, 0:1, :], rows_in.at[number, s : s + 1, :], partner)
             )
-        at += count
+        if number == 0:
+            finish_state()
         for copy in copies:
             copy.wait_recv()
         got = rows_in[number, 0:size, :]
@@ -586,23 +662,22 @@
             pltpu.VMEM((8, 128), jnp.int32),
             pltpu.VMEM((3, 8, 128), f32),
             pltpu.VMEM((8, 3, 8, 128), f32),
-            pltpu.VMEM((2, levels, 128), f32),
+            pltpu.VMEM((2, 2, levels, 128), f32),
             pltpu.VMEM((2, 2, 4, levels, 128), f32),
             pltpu.VMEM((2, 2, 4, levels, 128), f32),
             pltpu.VMEM((groups, 8, 128), f32),
             pltpu.VMEM((2, groups, 8, 128), f32),
             pltpu.VMEM((4, groups, 8, 128), f32),
             pltpu.VMEM((groups, 8, 128), f32),
-            pltpu.VMEM((2, 8, 128), f32),
-            pltpu.VMEM((8, 2, 8, 128), f32),
-            pltpu.VMEM((2, 8, 128), f32),
-            pltpu.VMEM((8, 2, 8, 128), f32),
+            pltpu.VMEM((groups, 8, 128), f32),
+            pltpu.VMEM((8, groups, 8, 128), f32),
+            pltpu.VMEM((4, 8, 128), f32),
+            pltpu.VMEM((8, 4, 8, 128), f32),
             pltpu.VMEM((2, 8, 128), f32),
             pltpu.VMEM((2, max(n_blocks, 16), 128), f32),
-            dma((8,)),
+            dma((10,)),
             dma((46 + n_sums,)),
-            dma((46,)),
-            dma((n_sums,)),
+            dma((46 + n_sums,)),
             pltpu.SemaphoreType.REGULAR((len(ROUNDS),)),
         ],
         compiler_params=pltpu.CompilerParams(collective_id=0, has_side_effects=True),

time: 46.5 us -> 43.4 us (0.933)
  Pallas kernels: 44.2 us -> 41.2 us
    pallas_call x1, Pallas kernels: 44.2 us -> 41.2 us  [on_device(): pl.pallas_call(functools.partial(kernel, n_blocks, n_group, inner), out_s...]
where the time goes in v3:
time: 43.4 us; the launch traced here: 43.2 us
  Pallas kernels  41.2 us (95%)
  local copies, waits for them, and re-layouts  1.41 us (3%)
  between operations  0.64 us (1%)
    pallas_call x1, Pallas kernels, on_device(): pl.pallas_call(functools.partial(kernel, n_blocks, n_group, inner), out_s...  41.2 us
    unnamed x2, local copies, waits for them, and re-layouts  1.41 us

profile of v3, /device:TPU:1, one launch (start us, length us, event | category | flops | bytes accessed | tf_op | source)
XLA Modules:
  0.0 43.2 jit_solution(11238312897109944484)
XLA Ops:
  0.6 41.2 %shard_map.59 = (f32[36,4,8,128]{3,2,1,0:T(8,128)S(1)}, f32[8,128]{1,0:T(8,128)S(1)}) custom-call(f32[36,4,8,128]{3,2,1,0:T(8,128)} %ocean.1, f32[8,128]{1,0:T(8,128)} %height.1, f32[8,128]{1,0:T(8,128)} %damping.1, s32[8,128]{1,0:T(8,128)} %land.1), custom_call_target="tpu_custom_call" | custom-call | tf_op jit(solution)/shard_map/pallas_call | solution.py:655
  41.8 0.8 %copy.8 = f32[36,4,8,128]{3,2,1,0:T(8,128)} copy(f32[36,4,8,128]{3,2,1,0:T(8,128)S(1)} %get-tuple-element.2) | data formatting | bytes 1179648
  42.6 0.6 %copy.9 = f32[8,128]{1,0:T(8,128)} copy(f32[8,128]{1,0:T(8,128)S(1)} %get-tuple-element.3) | data formatting | bytes 8192

commit v4 on v3

--- a/solution.py
+++ b/solution.py
@@ -19,10 +19,12 @@
 REACH = 1.125
 
 GROUP_LEVELS = 6
+FLOW_LEVELS = 12
 NEAR = ((-1, 0), (1, 0), (0, -1), (0, 1), (-1, -1), (-1, 1), (1, -1), (1, 1))
 OPPOSITE = (1, 0, 3, 2, 7, 6, 5, 4)
 UP, DOWN, LEFT, RIGHT, UP_LEFT, UP_RIGHT, DOWN_LEFT, DOWN_RIGHT = range(8)
-ROUNDS = ((1, 1), (2, 2), (1, 2))
+FIRST = ((1, 2, 3), (2, 3))
+ROUNDS = (((1, 2, 3), (3,)), ((1,), ()))
 
 
 def roll(x, shift, axis):
@@ -102,11 +104,12 @@
     ocean, height, damping, land,
     out, surface,
     own, sea_int, geo, geo_near, rows_own, rows_near, rows_fix, packed, packed_near, corner_near, packed_fix,
-    flow, flow_near, sums_own, sums_near, row_out, rows_in,
-    load_sems, send_sems, near_sems, greet_sems,
+    flow, flow_over, flow_side, flow_corner, sums_own, sums_near, rim, rim_near, row_out, rows_in,
+    load_sems, send_sems, near_sems, sum_sems, greet_sems,
 ):
     levels = ocean.shape[0]
     groups = levels // GROUP_LEVELS
+    flow_groups = levels // FLOW_LEVELS
     block = lax.axis_index("blocks")
     part = lax.axis_index("group")
     outer = n_blocks // inner
@@ -127,14 +130,12 @@
         return sorted(range(1, n), key=lambda s: -min(s, n - s))
 
     phases = [[along_blocks(s) for s in far_first(n_blocks)], [along_group(s) for s in far_first(n_group)]]
-    rounds = []
-    for rows_off, group_off in ROUNDS:
-        targets = []
-        if rows_off % outer:
-            targets += [along_blocks(rows_off * inner), along_blocks(-rows_off * inner)]
-        if group_off % n_group:
-            targets += [along_group(group_off), along_group(-group_off)]
-        rounds.append(targets)
+
+    def apart(rows, along):
+        found = [along_blocks(sign * d * inner) for d in rows if d % outer for sign in (1, -1)]
+        return found + [along_group(sign * d) for d in along if d % n_group for sign in (1, -1)]
+
+    rounds = [apart(*reach) for reach in ROUNDS]
 
     loads = [
         pltpu.make_async_copy(land, sea_int, load_sems.at[0]),
@@ -156,7 +157,7 @@
     partners = (
         [near(n) for n in range(8)]
         + [(base + lax.rem(block - base + s, inner), part) for s in range(1, inner)]
-        + ([along_blocks(inner), along_blocks(-inner)] if outer > 1 else [])
+        + apart(*FIRST)
     )
     for partner in partners:
         pl.semaphore_signal(barrier, inc=1, device_id=partner, device_id_type=MESH)
@@ -192,8 +193,6 @@
         sends.append(copy)
         return copy
 
-    pl.semaphore_wait(barrier, len(partners))
-
     def greet(n):
         for target in rounds[n]:
             pl.semaphore_signal(greet_sems.at[n], inc=1, device_id=target, device_id_type=MESH)
@@ -201,8 +200,6 @@
     def greeted(n):
         if rounds[n]:
             pl.semaphore_wait(greet_sems.at[n], len(rounds[n]))
-
-    greet(0)
 
     def send_rows(c, r):
         return [
@@ -210,31 +207,22 @@
             send(ocean.at[:, c, 7 - r, :], rows_near.at[0, r, c], near(DOWN)),
         ]
 
-    flow_rows = send_rows(2, 0) + send_rows(3, 0)
-
     for load in loads[:3]:
         load.wait()
     sea = sea_int[...].astype(jnp.float32)
     geo[0] = sea
-    shapes = [send(geo, geo_near.at[OPPOSITE[n]], near(n)) for n in range(8)]
 
     for load in loads[3:]:
         load.wait()
 
-    eighth = lax.rem(lane, 8)
-    sea_flow = jnp.where(lane < 8, roll(sea, 4, 1), 0.0)
-    for shift in (8, 16, 32, 64):
-        sea_flow = sea_flow + roll(sea_flow, shift, 1)
-    for group in range(groups):
-        held = [zero, zero, zero, zero]
-        for i in range(2 * GROUP_LEVELS):
-            field = own[group * GROUP_LEVELS + (i // 2 + 1), 2 + i % 2]
-            held[i % 4] = jnp.where(lane // 8 == i, roll(field, 4 + 8 * i, 1), held[i % 4])
-        flow[group] = ((held[0] + held[1]) + (held[2] + held[3])) * sea_flow
-    flows = []
-    for n in range(8):
-        rows = {-1: pl.ds(0, 4), 0: pl.ds(0, 8), 1: pl.ds(4, 4)}[NEAR[n][0]]
-        flows.append(send(flow.at[:, rows, :], flow_near.at[OPPOSITE[n], :, rows, :], near(n)))
+    for group in range(flow_groups):
+        west, east = [zero, zero], [zero, zero]
+        for i in range(2 * FLOW_LEVELS):
+            field = roll(own[group * FLOW_LEVELS + (i // 2 + 1), 2 + i % 2] * sea, 4 * i + 4, 1)
+            east[i % 2] = jnp.where(field_of == i, field, east[i % 2])
+            west[i % 2] = jnp.where(field_of == i + 1, field, west[i % 2])
+        flow[0, group] = roll(west[0] + west[1], -4, 1)
+        flow[1, group] = east[0] + east[1]
 
     not_first, not_last = flag(row > 0), flag(row < 7)
 
@@ -250,7 +238,31 @@
 
     for n, total in enumerate(lax.fori_loop(0, levels, advection, (zero, zero, zero, zero), unroll=4)):
         sums_own[n] = total
-    shared = [send(sums_own, sums_near.at[OPPOSITE[n]], near(n)) for n in range(8)]
+
+    held = zero
+    for n, plane in enumerate((sea, geo[1], geo[2], sums_own[0], sums_own[1], sums_own[2], sums_own[3])):
+        held = jnp.where(lane // 16 == n, roll(plane, 16 * n + 8, 1), held)
+    rim[...] = held
+
+    pl.semaphore_wait(barrier, len(partners))
+    greet(0)
+    halves = {-1: pl.ds(0, 4), 1: pl.ds(4, 4)}
+    beside = []
+    for n in (UP_LEFT, UP_RIGHT, DOWN_LEFT, DOWN_RIGHT):
+        rows, edge = halves[NEAR[n][0]], max(NEAR[n][1], 0)
+        beside.append(send(rim, rim_near.at[OPPOSITE[n] - 2], near(n)))
+        beside.append(
+            send(flow.at[edge, :, rows, :], flow_corner.at[OPPOSITE[n] - 4, :, rows, :], near(n))
+        )
+    for n in (DOWN, UP):
+        rows = halves[NEAR[n][0]]
+        beside.append(send(geo, geo_near.at[OPPOSITE[n]], near(n)))
+        beside.append(send(sums_own, sums_near.at[OPPOSITE[n]], near(n)))
+        beside.append(send(flow.at[:, :, rows, :], flow_over.at[OPPOSITE[n], :, :, rows, :], near(n)))
+    for n in (LEFT, RIGHT):
+        beside.append(send(rim, rim_near.at[OPPOSITE[n] - 2], near(n)))
+        beside.append(send(flow.at[max(NEAR[n][1], 0)], flow_side.at[OPPOSITE[n] - 2], near(n)))
+    flow_rows = send_rows(2, 0) + send_rows(3, 0)
 
     sea_packed = jnp.where(lane < 4, roll(sea, 2, 1), 0.0)
     for shift in (4, 8, 16, 32, 64):
@@ -274,9 +286,6 @@
     other_rows = send_rows(2, 1) + send_rows(3, 1)
     for c in (0, 1):
         other_rows += send_rows(c, 0) + send_rows(c, 1)
-    greeted(0)
-    greet(1)
-
     column = (part * 128 + lane).astype(jnp.float32)
     coriolis = (rotation * time_step) * (2.0 * (column + 0.5) / (128 * n_group) - 1.0)
     middle = 2.0 - jnp.where(first_row, 1.0 - has_up, 0.0) - jnp.where(last_row, 1.0 - has_down, 0.0)
@@ -312,50 +321,61 @@
 
     top = tuple(own[0, c] * sea for c in range(4))
     now = tuple(own[1, c] * sea for c in range(4))
-    lax.fori_loop(0, levels, step, (top, now))
-    greeted(1)
-    greet(2)
-
-    def around(mine, others):
-        low, west_half = row < 4, lane < 64
-        side = jnp.where(west_half, others[RIGHT], others[LEFT])
-        over = jnp.where(low, others[DOWN], others[UP])
-        corner = jnp.where(
-            low,
-            jnp.where(west_half, others[DOWN_RIGHT], others[DOWN_LEFT]),
-            jnp.where(west_half, others[UP_RIGHT], others[UP_LEFT]),
-        )
-        return jnp.concatenate(
-            [jnp.concatenate([mine, side], axis=1), jnp.concatenate([over, corner], axis=1)], axis=0
-        )
-
-    for copy in flow_rows + shapes + flows + shared:
+    half = levels // 2
+    middle_pair = lax.fori_loop(0, half, step, (top, now))
+    greeted(0)
+    greet(1)
+    lax.fori_loop(half, levels, step, middle_pair)
+
+    for copy in beside + flow_rows:
         copy.wait_recv()
 
-    sea_near = [geo_near[n, 0] * exists[n] for n in range(8)]
-    sea_all = around(sea, sea_near)
-    damping_all = around(geo[1], [geo_near[n, 1] for n in range(8)])
-    forced = sea_all * damping_all * around(geo[2], [geo_near[n, 2] for n in range(8)])
-
-    def around_whole(mine, others):
-        west_half = lane < 64
-        blocks = [
-            [mine, jnp.where(west_half, others[RIGHT], others[LEFT])],
-            [others[DOWN], jnp.where(west_half, others[DOWN_RIGHT], others[DOWN_LEFT])],
-            [others[UP], jnp.where(west_half, others[UP_RIGHT], others[UP_LEFT])],
-        ]
-        return jnp.concatenate([jnp.concatenate(b, axis=1) for b in blocks], axis=0)
+    low = row < 4
+    before = lax.rem(lane, 16) < 8
+    rims = [rim_near[n - 2] * exists[n] for n in range(2, 8)]
+    rim_side = jnp.where(before, rims[LEFT - 2], rims[RIGHT - 2])
+    rim_down = jnp.where(before, rims[DOWN_LEFT - 2], rims[DOWN_RIGHT - 2])
+    rim_up = jnp.where(before, rims[UP_LEFT - 2], rims[UP_RIGHT - 2])
+    rim_over = jnp.where(low, rim_down, rim_up)
+
+    def edge_of(x, plane):
+        return jnp.where((lane < 8) | (lane >= 120), roll(x, -(16 * plane + 8), 1), 0.0)
+
+    def stack(*pairs):
+        return jnp.concatenate([jnp.concatenate(pair, axis=1) for pair in pairs], axis=0)
+
+    def around(mine, up, down, plane):
+        return stack(
+            (mine, edge_of(rim_side, plane)), (jnp.where(low, down, up), edge_of(rim_over, plane))
+        )
+
+    sea_all = around(sea, geo_near[UP, 0] * has_up, geo_near[DOWN, 0] * has_down, 0)
+    damping_all = around(geo[1], geo_near[UP, 1], geo_near[DOWN, 1], 1)
+    forced = sea_all * damping_all * around(geo[2], geo_near[UP, 2], geo_near[DOWN, 2], 2)
+
+    def around_whole(m):
+        plane = m + 3
+        return stack(
+            (sums_own[m], edge_of(rim_side, plane)),
+            (sums_near[DOWN, m] * has_down, edge_of(rim_down, plane)),
+            (sums_near[UP, m] * has_up, edge_of(rim_up, plane)),
+        )
 
     def ring_laplace(x):
         return (roll(x, 1, 0) + roll(x, -1, 0)) + (roll(x, 1, 1) + roll(x, -1, 1)) - 4.0 * x
 
-    inside = around_whole(zero + 1.0, [zero + exists[n] for n in range(8)])
+    def beside_exists(left, right):
+        return jnp.where(lane < 64, zero + right, zero + left)
+
+    inside = stack(
+        (zero + 1.0, beside_exists(has_left, has_right)),
+        (zero + has_down, beside_exists(exists[DOWN_LEFT], exists[DOWN_RIGHT])),
+        (zero + has_up, beside_exists(exists[UP_LEFT], exists[UP_RIGHT])),
+    )
     ring_lane = lax.broadcasted_iota(jnp.int32, (24, 256), 1)
     ring_column = (part * 128 + jnp.where(ring_lane < 192, ring_lane, ring_lane - 256)).astype(jnp.float32)
     ring_coriolis = (rotation * time_step) * (2.0 * (ring_column + 0.5) / (128 * n_group) - 1.0)
-    level_sums = [
-        around_whole(sums_own[m], [sums_near[n, m] * exists[n] for n in range(8)]) for m in range(2)
-    ]
+    level_sums = [around_whole(m) for m in range(2)]
     linear = []
     for m in range(2):
         g = level_sums[m]
@@ -364,51 +384,62 @@
             + (ring_coriolis if m == 0 else -ring_coriolis) * level_sums[1 - m]
         )
 
-    flow_lane = lane // 8
-    is_east_field = lax.rem(flow_lane, 2) == 0
-    before_edge, after_edge = flag(eighth == 3), flag(eighth == 4)
+    is_east_field = lax.rem(field_of, 2) == 0
     first, last = flag(first_row), flag(last_row)
+    at_first, at_last = flag(quarter == 0), flag(quarter == 3)
 
     def of_u(x):
         x = jnp.where(is_east_field, x, 0.0)
-        return x + roll(x, 8, 1)
+        return x + roll(x, 4, 1)
 
     def of_v(x):
         x = jnp.where(is_east_field, 0.0, x)
-        return x + roll(x, -8, 1)
-
-    def across_columns(x, beside):
-        return of_v(x) * (before_edge * roll(beside, -1, 1) - after_edge * roll(beside, 1, 1))
+        return x + roll(x, -4, 1)
 
     def across_rows(x, beside):
         return of_u(x) * (last * roll(beside, -1, 0) - first * roll(beside, 1, 0))
 
-    gathered = [zero, zero, zero, zero]
-    for group in range(groups):
-        tiles = [flow_near[n, group] * exists[n] for n in range(8)]
-        low, ends = row < 4, eighth < 4
-        mine = flow[group]
-        over = jnp.where(low, tiles[DOWN], tiles[UP])
-        side = jnp.where(ends, tiles[LEFT], tiles[RIGHT])
-        over_side = jnp.where(
-            low,
-            jnp.where(ends, tiles[DOWN_LEFT], tiles[DOWN_RIGHT]),
-            jnp.where(ends, tiles[UP_LEFT], tiles[UP_RIGHT]),
-        )
-        gathered[0] = gathered[0] + across_columns(mine, side)
-        gathered[1] = gathered[1] + (across_columns(side, mine) + across_rows(side, over_side))
-        gathered[2] = gathered[2] + across_columns(over, over_side)
-        gathered[3] = gathered[3] + (across_columns(over_side, over) + across_rows(over_side, side))
-
-    def by_component(x, edge):
-        total = x
-        for l in range(1, GROUP_LEVELS):
-            total = total + roll(x, -16 * l, 1)
-        return [jnp.where(edge, roll(total, -(8 * c + 4), 1), 0.0) for c in range(2)]
-
-    at_edge = first_lane | last_lane
-    near_edge = (lane < 4) | (lane >= 124)
-    edges = [by_component(gathered[n], at_edge if n in (0, 2) else near_edge) for n in range(4)]
+    def meet_after(x, after):
+        return of_v(x) * (at_last * roll(after, 3, 1))
+
+    def meet_before(x, ahead):
+        return of_v(x) * (-at_first * roll(ahead, -3, 1))
+
+    gathered = [zero] * 8
+    for group in range(flow_groups):
+        mine = flow[0, group], flow[1, group]
+        over = [
+            jnp.where(low, flow_over[DOWN, e, group] * has_down, flow_over[UP, e, group] * has_up) for e in range(2)
+        ]
+        left, right = flow_side[0, group] * has_left, flow_side[1, group] * has_right
+        corner = [flow_corner[n - 4, group] * exists[n] for n in range(4, 8)]
+        over_left = jnp.where(low, corner[DOWN_LEFT - 4], corner[UP_LEFT - 4])
+        over_right = jnp.where(low, corner[DOWN_RIGHT - 4], corner[UP_RIGHT - 4])
+        terms = (
+            meet_before(mine[0], left),
+            meet_after(mine[1], right),
+            meet_before(right, mine[1]) + across_rows(right, over_right),
+            meet_after(left, mine[0]) + across_rows(left, over_left),
+            meet_before(over[0], over_left),
+            meet_after(over[1], over_right),
+            meet_before(over_right, over[1]) + across_rows(over_right, right),
+            meet_after(over_left, over[0]) + across_rows(over_left, left),
+        )
+        gathered = [a + b for a, b in zip(gathered, terms)]
+
+    def over_levels(x):
+        x = x + roll(x, -48, 1)
+        x = x + roll(x, -24, 1)
+        return x + (roll(x, -8, 1) + roll(x, -16, 1))
+
+    gathered = [over_levels(x) for x in gathered]
+
+    def placed(n, c):
+        return jnp.where(lane < 4, roll(gathered[n], -4 * c, 1), 0.0) + jnp.where(
+            lane >= 124, roll(gathered[n + 1], -4 * c - 4, 1), 0.0
+        )
+
+    edges = [[placed(2 * n, c) for c in range(2)] for n in range(4)]
 
     def met(x, g, weight):
         return jnp.broadcast_to(jnp.sum(x * g, axis=0, keepdims=True) * weight, (8, 128))
@@ -422,15 +453,10 @@
         outer_rows = last * met(rows_near[0, 0, 2], rows_own[0, m], above_weight) - first * met(
             rows_near[1, 0, 2], rows_own[1, m], below_weight
         )
-        crossing = jnp.concatenate(
-            [
-                jnp.concatenate([edges[0][m] + inner_rows, edges[1][m]], axis=1),
-                jnp.concatenate([edges[2][m] + outer_rows, edges[3][m]], axis=1),
-            ],
-            axis=0,
-        )
+        crossing = stack((edges[0][m] + inner_rows, edges[1][m]), (edges[2][m] + outer_rows, edges[3][m]))
         advected.append(
-            around(sums_own[2 + m], [sums_near[n, 2 + m] for n in range(8)]) + (0.5 * time_step) * crossing
+            around(sums_own[2 + m], sums_near[UP, 2 + m], sums_near[DOWN, 2 + m], 5 + m)
+            + (0.5 * time_step) * crossing
         )
 
     ring_low = lax.broadcasted_iota(jnp.int32, (8, 256), 0) < 4
@@ -573,20 +599,23 @@
         jnp.where(lane == row, total[0], jnp.where(lane == row + 64, total[1], 0.0)), axis=0, keepdims=True
     )
 
-    greeted(2)
+    greeted(1)
     for number, phase in enumerate(phases):
         count = len(phase)
         size = -(-(count + 1) // 8) * 8
         row_out[number, 0:1, :] = value
-        copies = []
         for s, partner in enumerate(phase):
-            copies.append(
-                send(row_out.at[number, 0:1, :], rows_in.at[number, s : s + 1, :], partner)
+            copy = pltpu.make_async_remote_copy(
+                src_ref=row_out.at[number, 0:1, :], dst_ref=rows_in.at[number, s : s + 1, :],
+                send_sem=send_sems.at[len(sends)], recv_sem=sum_sems.at[number],
+                device_id=partner, device_id_type=MESH,
             )
+            copy.start()
+            sends.append(copy)
         if number == 0:
             finish_state()
-        for copy in copies:
-            copy.wait_recv()
+        whole = rows_in.at[number, 0:count, :]
+        pltpu.make_async_copy(whole, whole, sum_sems.at[number]).wait()
         got = rows_in[number, 0:size, :]
         row_number = lax.broadcasted_iota(jnp.int32, (size, 128), 0)
         got = jnp.where(row_number < count, got, jnp.where(row_number == count, row_out[number, 0:1, :], 0.0))
@@ -647,6 +676,7 @@
 def on_device(n_blocks, n_group, inner, ocean_state, surface_height, surface_damping, land_mask):
     levels = ocean_state.shape[0]
     groups = levels // GROUP_LEVELS
+    flow_groups = levels // FLOW_LEVELS
     f32 = jnp.float32
     any_space = pl.BlockSpec(memory_space=pl.ANY)
     vmem = pl.BlockSpec(memory_space=pltpu.VMEM)
@@ -661,7 +691,7 @@
             pltpu.VMEM((levels + 2, 4, 8, 128), f32),
             pltpu.VMEM((8, 128), jnp.int32),
             pltpu.VMEM((3, 8, 128), f32),
-            pltpu.VMEM((8, 3, 8, 128), f32),
+            pltpu.VMEM((2, 3, 8, 128), f32),
             pltpu.VMEM((2, 2, levels, 128), f32),
             pltpu.VMEM((2, 2, 4, levels, 128), f32),
             pltpu.VMEM((2, 2, 4, levels, 128), f32),
@@ -669,15 +699,20 @@
             pltpu.VMEM((2, groups, 8, 128), f32),
             pltpu.VMEM((4, groups, 8, 128), f32),
             pltpu.VMEM((groups, 8, 128), f32),
-            pltpu.VMEM((groups, 8, 128), f32),
-            pltpu.VMEM((8, groups, 8, 128), f32),
+            pltpu.VMEM((2, flow_groups, 8, 128), f32),
+            pltpu.VMEM((2, 2, flow_groups, 8, 128), f32),
+            pltpu.VMEM((2, flow_groups, 8, 128), f32),
+            pltpu.VMEM((4, flow_groups, 8, 128), f32),
             pltpu.VMEM((4, 8, 128), f32),
-            pltpu.VMEM((8, 4, 8, 128), f32),
+            pltpu.VMEM((2, 4, 8, 128), f32),
+            pltpu.VMEM((8, 128), f32),
+            pltpu.VMEM((6, 8, 128), f32),
             pltpu.VMEM((2, 8, 128), f32),
             pltpu.VMEM((2, max(n_blocks, 16), 128), f32),
             dma((10,)),
-            dma((46 + n_sums,)),
-            dma((46 + n_sums,)),
+            dma((40 + n_sums,)),
+            dma((40,)),
+            dma((2,)),
             pltpu.SemaphoreType.REGULAR((len(ROUNDS),)),
         ],
         compiler_params=pltpu.CompilerParams(collective_id=0, has_side_effects=True),

time: 43.4 us -> 41.9 us (0.965)
  Pallas kernels: 41.2 us -> 39.7 us
    pallas_call x1, Pallas kernels: 41.2 us -> 39.7 us  [on_device(): pl.pallas_call(functools.partial(kernel, n_blocks, n_group, inner), out_s...]
where the time goes in v4:
time: 41.9 us; the launch traced here: 41.8 us
  Pallas kernels  39.7 us (95%)
  local copies, waits for them, and re-layouts  1.41 us (3%)
  between operations  0.64 us (2%)
    pallas_call x1, Pallas kernels, on_device(): pl.pallas_call(functools.partial(kernel, n_blocks, n_group, inner), out_s...  39.7 us
    unnamed x2, local copies, waits for them, and re-layouts  1.41 us

profile of v4, /device:TPU:1, one launch (start us, length us, event | category | flops | bytes accessed | tf_op | source)
XLA Modules:
  0.0 41.8 jit_solution(17583689232380306229)
XLA Ops:
  0.6 39.7 %shard_map.59 = (f32[36,4,8,128]{3,2,1,0:T(8,128)S(1)}, f32[8,128]{1,0:T(8,128)S(1)}) custom-call(f32[36,4,8,128]{3,2,1,0:T(8,128)} %ocean.1, f32[8,128]{1,0:T(8,128)} %height.1, f32[8,128]{1,0:T(8,128)} %damping.1, s32[8,128]{1,0:T(8,128)} %land.1), custom_call_target="tpu_custom_call" | custom-call | tf_op jit(solution)/shard_map/pallas_call | solution.py:685
  40.3 0.8 %copy.8 = f32[36,4,8,128]{3,2,1,0:T(8,128)} copy(f32[36,4,8,128]{3,2,1,0:T(8,128)S(1)} %get-tuple-element.2) | data formatting | bytes 1179648
  41.2 0.6 %copy.9 = f32[8,128]{1,0:T(8,128)} copy(f32[8,128]{1,0:T(8,128)S(1)} %get-tuple-element.3) | data formatting | bytes 8192

commit v5 on v4

--- a/solution.py
+++ b/solution.py
@@ -682,7 +682,7 @@
     vmem = pl.BlockSpec(memory_space=pltpu.VMEM)
     n_sums = (n_blocks - 1) + (n_group - 1)
     dma = pltpu.SemaphoreType.DMA
-    return pl.pallas_call(
+    new_state, surface = pl.pallas_call(
         functools.partial(kernel, n_blocks, n_group, inner),
         out_shape=(pltpu.VMEM(ocean_state.shape, f32), pltpu.VMEM(surface_height.shape, f32)),
         in_specs=[any_space] * 4,
@@ -717,6 +717,32 @@
         ],
         compiler_params=pltpu.CompilerParams(collective_id=0, has_side_effects=True),
     )(ocean_state, surface_height, surface_damping, land_mask)
+    return pl.pallas_call(
+        put_out,
+        out_shape=(
+            jax.ShapeDtypeStruct(ocean_state.shape, f32),
+            jax.ShapeDtypeStruct(surface_height.shape, f32),
+        ),
+        in_specs=[any_space, any_space],
+        out_specs=(any_space, any_space),
+        scratch_shapes=[dma((3,))],
+    )(
+        pltpu.with_memory_space_constraint(new_state, pltpu.VMEM),
+        pltpu.with_memory_space_constraint(surface, pltpu.VMEM),
+    )
+
+
+def put_out(state, surface, state_out, surface_out, sems):
+    half = state.shape[0] // 2
+    copies = (
+        pltpu.make_async_copy(state.at[:half], state_out.at[:half], sems.at[0]),
+        pltpu.make_async_copy(state.at[half:], state_out.at[half:], sems.at[1]),
+        pltpu.make_async_copy(surface, surface_out, sems.at[2]),
+    )
+    for copy in copies:
+        copy.start()
+    for copy in copies:
+        copy.wait()
 
 
 def solution(mesh):

time: 41.9 us -> 41.3 us (0.986)
  local copies, waits for them, and re-layouts: 1.41 us -> 0 us
  Pallas kernels: 39.7 us -> 40.6 us
    unnamed x2 -> x0, local copies, waits for them, and re-layouts: 1.41 us -> none
    pallas_call x0 -> x1, Pallas kernels: none -> 0.84 us  [on_device(): pl.pallas_call(put_out, out_shape=(jax.ShapeDtypeStruct(ocean_state.shape...]
where the time goes in v5:
time: 41.3 us; the launch traced here: 41.2 us
  Pallas kernels  40.6 us (98%)
  between operations  0.64 us (2%)
    pallas_call x1, Pallas kernels, on_device(): pl.pallas_call(functools.partial(kernel, n_blocks, n_group, inner), out_s...  39.7 us
    pallas_call x1, Pallas kernels, on_device(): pl.pallas_call(put_out, out_shape=(jax.ShapeDtypeStruct(ocean_state.shape...  0.84 us

profile of v5, /device:TPU:1, one launch (start us, length us, event | category | flops | bytes accessed | tf_op | source)
XLA Modules:
  0.0 41.2 jit_solution(14640080601535312373)
XLA Ops:
  0.6 39.7 %shard_map.59 = (f32[36,4,8,128]{3,2,1,0:T(8,128)S(1)}, f32[8,128]{1,0:T(8,128)S(1)}) custom-call(f32[36,4,8,128]{3,2,1,0:T(8,128)} %ocean.1, f32[8,128]{1,0:T(8,128)} %height.1, f32[8,128]{1,0:T(8,128)} %damping.1, s32[8,128]{1,0:T(8,128)} %land.1), custom_call_target="tpu_custom_call" | custom-call | tf_op jit(solution)/shard_map/pallas_call | solution.py:685
  40.3 0.8 %shard_map.60 = (f32[36,4,8,128]{3,2,1,0:T(8,128)}, f32[8,128]{1,0:T(8,128)}) custom-call(f32[36,4,8,128]{3,2,1,0:T(8,128)S(1)} %get-tuple-element.4.state, f32[8,128]{1,0:T(8,128)S(1)} %get-tuple-element.5.surface), custom_call_target="tpu_custom_call" | custom-call | tf_op jit(solution)/shard_map/pallas_call | solution.py:720

commit v6 on v5

--- a/solution.py
+++ b/solution.py
@@ -319,13 +319,13 @@
             out[level, c] = new
         return now, below
 
-    top = tuple(own[0, c] * sea for c in range(4))
-    now = tuple(own[1, c] * sea for c in range(4))
-    half = levels // 2
-    middle_pair = lax.fori_loop(0, half, step, (top, now))
+    def step_alone():
+        top = tuple(own[0, c] * sea for c in range(4))
+        now = tuple(own[1, c] * sea for c in range(4))
+        lax.fori_loop(0, levels, step, (top, now))
+
     greeted(0)
     greet(1)
-    lax.fori_loop(half, levels, step, middle_pair)
 
     for copy in beside + flow_rows:
         copy.wait_recv()
@@ -474,7 +474,10 @@
     divergence = 0.5 * (roll(east_all, -1, 0) - roll(east_all, 1, 0) + roll(north_all, -1, 1) - roll(north_all, 1, 1))
     v0 = forced - (gravity * sea_all) * divergence
 
-    def finish_state():
+    beside_edges = (lane < 2) | (lane >= 126)
+
+    def start_state():
+        step_alone()
         own_flow = []
         for group in range(groups):
             north = jnp.where(lax.rem(field_of, 4) == 3, packed[group], 0.0)
@@ -529,12 +532,12 @@
             )
             return fixed * sea_packed
 
-        beside_edges = (lane < 2) | (lane >= 126)
         for group in range(groups):
             packed_fix[group] = fix_columns(group)
         for c in range(4):
             fix_rows(c)
 
+    def finish_state():
         def finish(group, carry):
             def at_corner(n):
                 return jnp.broadcast_to(corner_near[n - 4, group, 0:1, :] * exists[n], (8, 128))
@@ -613,6 +616,8 @@
             copy.start()
             sends.append(copy)
         if number == 0:
+            start_state()
+        else:
             finish_state()
         whole = rows_in.at[number, 0:count, :]
         pltpu.make_async_copy(whole, whole, sum_sems.at[number]).wait()

time: 41.3 us -> 38.1 us (0.923)
  Pallas kernels: 40.6 us -> 37.4 us
    pallas_call x1, Pallas kernels: 39.7 us -> 36.5 us  [on_device(): pl.pallas_call(functools.partial(kernel, n_blocks, n_group, inner), out_s...]
where the time goes in v6:
time: 38.1 us; the launch traced here: 38 us
  Pallas kernels  37.4 us (98%)
  between operations  0.64 us (2%)
    pallas_call x1, Pallas kernels, on_device(): pl.pallas_call(functools.partial(kernel, n_blocks, n_group, inner), out_s...  36.5 us
    pallas_call x1, Pallas kernels, on_device(): pl.pallas_call(put_out, out_shape=(jax.ShapeDtypeStruct(ocean_state.shape...  0.84 us

profile of v6, /device:TPU:1, one launch (start us, length us, event | category | flops | bytes accessed | tf_op | source)
XLA Modules:
  0.0 38.0 jit_solution(8268198155796380075)
XLA Ops:
  0.6 36.5 %shard_map.59 = (f32[36,4,8,128]{3,2,1,0:T(8,128)S(1)}, f32[8,128]{1,0:T(8,128)S(1)}) custom-call(f32[36,4,8,128]{3,2,1,0:T(8,128)} %ocean.1, f32[8,128]{1,0:T(8,128)} %height.1, f32[8,128]{1,0:T(8,128)} %damping.1, s32[8,128]{1,0:T(8,128)} %land.1), custom_call_target="tpu_custom_call" | custom-call | tf_op jit(solution)/shard_map/pallas_call | solution.py:690
  37.1 0.8 %shard_map.60 = (f32[36,4,8,128]{3,2,1,0:T(8,128)}, f32[8,128]{1,0:T(8,128)}) custom-call(f32[36,4,8,128]{3,2,1,0:T(8,128)S(1)} %get-tuple-element.4.state, f32[8,128]{1,0:T(8,128)S(1)} %get-tuple-element.5.surface), custom_call_target="tpu_custom_call" | custom-call | tf_op jit(solution)/shard_map/pallas_call | solution.py:725

commit v7 on v6

--- a/solution.py
+++ b/solution.py
@@ -322,7 +322,7 @@
     def step_alone():
         top = tuple(own[0, c] * sea for c in range(4))
         now = tuple(own[1, c] * sea for c in range(4))
-        lax.fori_loop(0, levels, step, (top, now))
+        lax.fori_loop(0, levels, step, (top, now), unroll=2)
 
     greeted(0)
     greet(1)

time: 38.1 us -> 38.1 us (level)
  no operation moved by 1% of the time
where the time goes in v7:
time: 38.1 us; the launch traced here: 38 us
  Pallas kernels  37.4 us (98%)
  between operations  0.64 us (2%)
    pallas_call x1, Pallas kernels, on_device(): pl.pallas_call(functools.partial(kernel, n_blocks, n_group, inner), out_s...  36.5 us
    pallas_call x1, Pallas kernels, on_device(): pl.pallas_call(put_out, out_shape=(jax.ShapeDtypeStruct(ocean_state.shape...  0.84 us

profile of v7, /device:TPU:1, one launch (start us, length us, event | category | flops | bytes accessed | tf_op | source)
XLA Modules:
  0.0 38.0 jit_solution(12948962464617458678)
XLA Ops:
  0.6 36.5 %shard_map.59 = (f32[36,4,8,128]{3,2,1,0:T(8,128)S(1)}, f32[8,128]{1,0:T(8,128)S(1)}) custom-call(f32[36,4,8,128]{3,2,1,0:T(8,128)} %ocean.1, f32[8,128]{1,0:T(8,128)} %height.1, f32[8,128]{1,0:T(8,128)} %damping.1, s32[8,128]{1,0:T(8,128)} %land.1), custom_call_target="tpu_custom_call" | custom-call | tf_op jit(solution)/shard_map/pallas_call | solution.py:690
  37.1 0.8 %shard_map.60 = (f32[36,4,8,128]{3,2,1,0:T(8,128)}, f32[8,128]{1,0:T(8,128)}) custom-call(f32[36,4,8,128]{3,2,1,0:T(8,128)S(1)} %get-tuple-element.4.state, f32[8,128]{1,0:T(8,128)S(1)} %get-tuple-element.5.surface), custom_call_target="tpu_custom_call" | custom-call | tf_op jit(solution)/shard_map/pallas_call | solution.py:725
